TPU v7x, 32 devices: a whole 2x2x4 slice. The times are simulated.
32 devices in a mesh: head: 4 (over x, core), ctx: 8 (over z, y).
Axes of the slice: x: 2, y: 2, z: 4, core: 2. Of those that a mesh axis runs over, the one named last changes fastest.
Arguments:
- query: bfloat16 [8, 512, 512], P('ctx', 'head'), may hold values from -36 to 36
- key: bfloat16 [8, 512, 512], P('ctx', 'head'), may hold values from -36 to 36
- value: bfloat16 [8, 512, 512], P('ctx', 'head'), may hold values from -6 to 6
- resid_in: bfloat16 [8, 512, 1024], P('ctx', 'head'), may hold values from -6 to 6
- out_grad: bfloat16 [8, 512, 1024], P('ctx', 'head'), may hold values from -6 to 6
- out_weight: bfloat16 [512, 1024], replicated, may hold values from -0.25 to 0.25
- conv_kernel: bfloat16 [31, 1024], replicated, may hold values from -1 to 1
- frame_lengths: int32 [8], replicated, may hold values from 256 to 512, as said below
Outputs:
- d_resid: bfloat16 [8, 512, 1024], P('ctx', None, 'head')
- d_query: bfloat16 [8, 512, 512], P('ctx', None, 'head')
- d_key: bfloat16 [8, 512, 512], P('ctx', None, 'head')
- d_value: bfloat16 [8, 512, 512], P('ctx', None, 'head')
Inputs may be any that keep to these rules, and one draw needn't show every extreme that they name: Block b holds audio in its first frame_lengths[b] frames; at least one block is full.
All inputs are finite; a program needn't handle non-finite values.
Results may differ from a plain program's by a relative error of at most 0.0086.
Values may be sent and summed in bfloat16 or wider, within the bound.
No kernel may reach another device: no remote copies, remote signals or barrier semaphores. Data moves between devices by JAX's collectives and lax.ppermute only.
A program may use at most 128 MiB of HBM per device.

v0:
```python
import jax
import jax.numpy as jnp
from jax import lax
from jax.sharding import PartitionSpec as P

HEAD_DIM = 64
KERNEL = 31
REACH = 2


def padded(cells, sides, width):
    for axis, dim in sides:
        count = lax.axis_size(axis)
        ends = count - 1
        head = lax.slice_in_dim(cells, 0, width, axis=dim)
        tail = lax.slice_in_dim(cells, cells.shape[dim] - width, cells.shape[dim], axis=dim)
        cells = jnp.concatenate(
            [
                lax.ppermute(tail, axis, [(i, (i + 1) % count) for i in range(ends)]),
                cells,
                lax.ppermute(head, axis, [((i + 1) % count, i) for i in range(ends)]),
            ],
            axis=dim,
        )
    return cells


def shifted(value, axis, steps):
    count = lax.axis_size(axis)
    first, last = (max(0, -steps), min(count, count - steps))
    return lax.ppermute(value, axis, [(source, source + steps) for source in range(first, last)])


def swish_slope(before):
    logistic = jax.nn.sigmoid(before)
    return logistic * (1.0 + before * (1.0 - logistic))


def conv_backward(resid_wide, grad_wide, weights_here, frames_here):
    margin = (KERNEL - 1) // 2
    channels = resid_wide.shape[1]
    extent = frames_here + 2 * margin
    conv_pre = jnp.zeros((extent, channels), jnp.float32)
    for offset in range(KERNEL):
        conv_pre = conv_pre + weights_here[offset] * resid_wide[offset : offset + extent]
    conv_grad = grad_wide[margin : margin + extent] * swish_slope(conv_pre)
    total = grad_wide[2 * margin : 2 * margin + frames_here]
    for offset in range(KERNEL):
        start_at = 2 * margin - offset
        total = total + weights_here[offset] * conv_grad[start_at : start_at + frames_here]
    return total.astype(jnp.bfloat16)


def on_device(query, key, value, resid_in, out_grad, out_weight, conv_kernel, frame_lengths):
    margin = (KERNEL - 1) // 2
    reach_rows = 2 * margin
    head_place = lax.axis_index("head")
    moved = (
        lax.all_to_all(query, "head", split_axis=2, concat_axis=1, tiled=True),
        lax.all_to_all(key, "head", split_axis=2, concat_axis=1, tiled=True),
        lax.all_to_all(value, "head", split_axis=2, concat_axis=1, tiled=True),
        lax.all_to_all(resid_in, "head", split_axis=2, concat_axis=1, tiled=True),
        lax.all_to_all(out_grad, "head", split_axis=2, concat_axis=1, tiled=True),
    )
    query_rows = moved[0][0]
    key_rows = moved[1][0]
    value_rows = moved[2][0]
    resid_rows = moved[3][0]
    grad_rows = moved[4][0]
    block_frames = resid_rows.shape[0]
    channels = resid_rows.shape[1]
    weights_here = lax.dynamic_slice_in_dim(conv_kernel, head_place * channels, channels, 1).astype(
        jnp.float32
    )
    resid_ext, grad_ext = (
        padded(resid_rows, (("ctx", 0),), reach_rows),
        padded(grad_rows, (("ctx", 0),), reach_rows),
    )
    d_resid = conv_backward(
        resid_ext.astype(jnp.float32), grad_ext.astype(jnp.float32), weights_here, block_frames
    )
    width_cols = query_rows.shape[1]
    weight_rows = lax.dynamic_slice_in_dim(out_weight, head_place * width_cols, width_cols, 0)
    head_sum = lax.dot_general(
        lax.all_gather(d_resid, "head", axis=1, tiled=True),
        weight_rows,
        (((1,), (1,)), ((), ())),
        preferred_element_type=jnp.float32,
    )
    head_grad = head_sum.astype(jnp.bfloat16)
    d_resid_out = d_resid[None]
    frames_here = query_rows.shape[0]
    width_here = query_rows.shape[1]
    heads_here = width_here // HEAD_DIM
    scale = HEAD_DIM ** (-0.5)
    query_heads = query_rows.reshape(frames_here, heads_here, HEAD_DIM)
    grad_heads = head_grad.reshape(frames_here, heads_here, HEAD_DIM)
    block_place = lax.axis_index("ctx")
    block_count = frame_lengths.shape[0]
    window = REACH * frames_here
    local_rows = jnp.arange(frames_here, dtype=jnp.int32)
    query_place = block_place * frames_here + local_rows

    def live_mask(offset):
        neighbour = block_place + offset
        key_place = neighbour * frames_here + local_rows
        limit = frame_lengths[jnp.clip(neighbour, 0, block_count - 1)]
        inside = (neighbour >= 0) & (neighbour < block_count)
        near = jnp.abs(query_place[:, None] - key_place[None, :]) <= window
        return near & (local_rows[None, :] < limit) & inside

    fetched = {0: (key_rows, value_rows)}
    for direction in (1, -1):
        last_key, last_value = (key_rows, value_rows)
        for distance in range(1, REACH + 1):
            send_key = last_key
            send_value = last_value
            last_key, last_value = shifted((send_key, send_value), "ctx", direction)
            fetched[-direction * distance] = (last_key, last_value)
    order = [0] + [offset for offset in range(-REACH, REACH + 1) if offset != 0]

    def block_logits(offset):
        keys_now = fetched[offset][0].reshape(frames_here, heads_here, HEAD_DIM)
        raw = (
            jnp.einsum("qhd,khd->hqk", query_heads, keys_now, preferred_element_type=jnp.float32)
            * scale
        )
        return jnp.where(live_mask(offset)[None], raw, -jnp.inf)

    def block_slopes(offset):
        values_now = fetched[offset][1].reshape(frames_here, heads_here, HEAD_DIM)
        return jnp.einsum(
            "qhd,khd->hqk", grad_heads, values_now, preferred_element_type=jnp.float32
        )

    for offset in order:
        logits = block_logits(offset)
        slopes = block_slopes(offset)
        if offset == 0:
            highest = jnp.max(logits, axis=2)
            scaled = jnp.exp(logits - highest[:, :, None])
            mass = jnp.sum(scaled, axis=2)
            weighted = jnp.sum(scaled * slopes, axis=2)
        else:
            fresh = jnp.maximum(highest, jnp.max(logits, axis=2))
            factor = jnp.exp(highest - fresh)
            scaled = jnp.exp(logits - fresh[:, :, None])
            mass = mass * factor + jnp.sum(scaled, axis=2)
            weighted = weighted * factor + jnp.sum(scaled * slopes, axis=2)
            highest = fresh
    log_total = highest + jnp.log(mass)
    delta = weighted / mass
    query_grad = jnp.zeros((frames_here, heads_here, HEAD_DIM), jnp.float32)
    for offset in order:
        keys_now = fetched[offset][0].reshape(frames_here, heads_here, HEAD_DIM)
        logits = block_logits(offset)
        probs = jnp.exp(logits - log_total[:, :, None])
        slopes = block_slopes(offset)
        dlogits = (probs * (slopes - delta[:, :, None])).astype(jnp.bfloat16)
        probs_low = probs.astype(jnp.bfloat16)
        query_grad = (
            query_grad
            + jnp.einsum("hqk,khd->qhd", dlogits, keys_now, preferred_element_type=jnp.float32)
            * scale
        )
        key_part = (
            (
                jnp.einsum("hqk,qhd->khd", dlogits, query_heads, preferred_element_type=jnp.float32)
                * scale
            )
            .astype(jnp.bfloat16)
            .reshape(frames_here, width_here)
        )
        value_part = (
            jnp.einsum("hqk,qhd->khd", probs_low, grad_heads, preferred_element_type=jnp.float32)
            .astype(jnp.bfloat16)
            .reshape(frames_here, width_here)
        )
        if offset == 0:
            key_total = key_part.astype(jnp.float32)
            value_total = value_part.astype(jnp.float32)
        else:
            back_key, back_value = shifted((key_part, value_part), "ctx", offset)
            key_total = key_total + back_key.astype(jnp.float32)
            value_total = value_total + back_value.astype(jnp.float32)
    return (
        d_resid_out,
        query_grad.reshape(frames_here, width_here).astype(jnp.bfloat16)[None],
        key_total.astype(jnp.bfloat16)[None],
        value_total.astype(jnp.bfloat16)[None],
    )


def solution(mesh):
    in_specs = (
        P("ctx", "head", None),
        P("ctx", "head", None),
        P("ctx", "head", None),
        P("ctx", "head", None),
        P("ctx", "head", None),
        P(),
        P(),
        P(),
    )
    out_specs = (
        P("ctx", None, "head"),
        P("ctx", None, "head"),
        P("ctx", None, "head"),
        P("ctx", None, "head"),
    )
    return jax.shard_map(
        on_device, mesh=mesh, in_specs=in_specs, out_specs=out_specs, check_vma=False
    )
```

profile of v0, /device:TPU:14, one launch (start us, length us, event | category | flops | bytes accessed | tf_op | source)
XLA Modules:
  0.0 204.8 jit_solution(15611372679468310429)
XLA Ops:
  7.2 1.2 copy.117
  8.9 1.4 reduce.3
  11.0 3.8 %all-to-all-start.2 = ((bf16[4,2,8192]{2,1,0:T(2,128)(2,1)}), bf16[4,2,8192]{2,1,0:T(2,128)(2,1)S(1)}, u32[]{:S(2)}, u32[]{:S(2)}) async-start(bf16[4,2,8192]{2,1,0:T(2,128)(2,1)} %reshape.507), calls=%async_computation.2 | async-start | bytes 262144 | tf_op jit(solution)/shard_map/all_to_all | solution.py:59
  14.8 1.5 fusion.111
  17.0 1.3 iota_compare_fusion.2
  18.3 1.3 iota_compare_fusion
  19.6 3.0 %fusion.33 = (pred[512,512]{0,1:T(8,128)(4,1)}, pred[512,512]{0,1:T(8,128)(4,1)}, pred[512,512]{0,1:T(8,128)(4,1)}, pred[512,512]{0,1:T(8,128)(4,1)}, pred[512,512]{0,1:T(8,128)(4,1)}) fusion(s32[512]{0:T(512)S(1)} %get-tuple-element.108, s32[512]{0:T(512)S(1)} %iota_add_fusion.4, pred[512]{0:T(512)(128)(4,1)S(1)} %get-tuple-element.106, pred[]{:T(512)S(6)} %and.169, ...), kind=kLoop, calls=%fused_computation.72 | loop fusion | flops 6553600 | bytes 1323525 | tf_op jit(solution)/shard_map/and | solution.py:110
  22.8 1.4 reduce.2
  25.0 1.4 reduce.4
  27.2 3.4 %all-to-all-start.3 = ((bf16[4,2,8192]{2,1,0:T(2,128)(2,1)}), bf16[4,2,8192]{2,1,0:T(2,128)(2,1)S(1)}, u32[]{:S(2)}, u32[]{:S(2)}) async-start(bf16[4,2,8192]{2,1,0:T(2,128)(2,1)} %reshape.503), calls=%async_computation.3 | async-start | bytes 262144 | tf_op jit(solution)/shard_map/all_to_all | solution.py:60
  31.3 2.2 %all-to-all-done.3 = bf16[4,2,8192]{2,1,0:T(2,128)(2,1)S(1)} async-done(((bf16[4,2,8192]{2,1,0:T(2,128)(2,1)}), bf16[4,2,8192]{2,1,0:T(2,128)(2,1)S(1)}, u32[]{:S(2)}, u32[]{:S(2)}) %all-to-all-start.3) | async-done | bytes 131104 | tf_op jit(solution)/shard_map/all_to_all | solution.py:60
  33.5 5.0 %all-to-all-start.4 = ((bf16[4,2,8192]{2,1,0:T(2,128)(2,1)}), bf16[4,2,8192]{2,1,0:T(2,128)(2,1)S(1)}, u32[]{:S(2)}, u32[]{:S(2)}) async-start(bf16[4,2,8192]{2,1,0:T(2,128)(2,1)} %reshape.505), calls=%async_computation.4 | async-start | bytes 262144 | tf_op jit(solution)/shard_map/all_to_all | solution.py:61
  38.9 2.2 %reduce.1 = bf16[1024,128]{1,0:T(8,128)(2,1)S(1)} reduce(bf16[1024,1,128]{2,1,0:T(2,128)(2,1)S(1)} %bitcast.177, bf16[]{:T(256)} %broadcast.279), dimensions={1}, to_apply=%bitcast.110.reduce_sub_computation | reduce | bytes 524290
  42.3 2.2 %reduce = bf16[1024,128]{1,0:T(8,128)(2,1)S(1)} reduce(bf16[1024,1,128]{2,1,0:T(2,128)(2,1)S(1)} %bitcast.176, bf16[]{:T(256)} %broadcast.279), dimensions={1}, to_apply=%bitcast.108.reduce_sub_computation | reduce | bytes 524290
  45.3 3.4 %all-to-all-start.1 = ((bf16[4,2,16384]{2,1,0:T(2,128)(2,1)}), bf16[4,2,16384]{2,1,0:T(2,128)(2,1)S(1)}, u32[]{:S(2)}, u32[]{:S(2)}) async-start(bf16[4,2,16384]{2,1,0:T(2,128)(2,1)} %reshape.501), calls=%async_computation.1 | async-start | bytes 524288 | tf_op jit(solution)/shard_map/all_to_all | solution.py:62
  49.7 2.4 %collective-permute-start.6 = (bf16[512,128]{1,0:T(8,128)(2,1)}, bf16[512,128]{1,0:T(8,128)(2,1)}, u32[]{:S(2)}, u32[]{:S(2)}) collective-permute-start(bf16[512,128]{1,0:T(8,128)(2,1)} %bitcast.40), channel_id=1, source_target_pairs={{1,0},{2,1},{3,2},{4,3},{5,4},{6,5},{7,6},{9,8},{10,9},{11,10},{12... | collective-permute-start | bytes 393224 | tf_op jit(solution)/shard_map/ppermute | solution.py:31
  52.2 4.3 %collective-permute-start.4 = (bf16[512,128]{1,0:T(8,128)(2,1)}, bf16[512,128]{1,0:T(8,128)(2,1)}, u32[]{:S(2)}, u32[]{:S(2)}) collective-permute-start(bf16[512,128]{1,0:T(8,128)(2,1)} %bitcast.40), channel_id=1, source_target_pairs={{0,1},{1,2},{2,3},{3,4},{4,5},{5,6},{6,7},{8,9},{9,10},{10,11},{11... | collective-permute-start | bytes 393224 | tf_op jit(solution)/shard_map/ppermute | solution.py:31
  57.8 1.9 collective-permute-start.10
  59.8 3.4 %all-to-all-start = ((bf16[4,2,16384]{2,1,0:T(2,128)(2,1)}), bf16[4,2,16384]{2,1,0:T(2,128)(2,1)S(1)}, u32[]{:S(2)}, u32[]{:S(2)}) async-start(bf16[4,2,16384]{2,1,0:T(2,128)(2,1)} %reshape.499), calls=%async_computation | async-start | bytes 524288 | tf_op jit(solution)/shard_map/all_to_all | solution.py:63
  63.7 4.8 %collective-permute-start.2 = (bf16[30,256]{1,0:T(8,128)(2,1)S(1)}, bf16[30,256]{1,0:T(8,128)(2,1)S(1)}, u32[]{:S(2)}, u32[]{:S(2)}) collective-permute-start(bf16[30,256]{1,0:T(8,128)(2,1)S(1)} %get-tuple-element.36), channel_id=1, source_target_pairs={{0,1},{1,2},{2,3},{3,4},{4,5},{5,6},{6,7},{8,9},{9,10},{10,11},{11... | collective-permute-start | bytes 46088 | tf_op jit(solution)/shard_map/ppermute | solution.py:19
  68.6 1.9 collective-permute-start.3
  71.0 4.8 %collective-permute-start = (bf16[30,256]{1,0:T(8,128)(2,1)S(1)}, bf16[30,256]{1,0:T(8,128)(2,1)S(1)}, u32[]{:S(2)}, u32[]{:S(2)}) collective-permute-start(bf16[30,256]{1,0:T(8,128)(2,1)S(1)} %get-tuple-element.38), channel_id=1, source_target_pairs={{0,1},{1,2},{2,3},{3,4},{4,5},{5,6},{6,7},{8,9},{9,10},{10,11},{11... | collective-permute-start | bytes 46088 | tf_op jit(solution)/shard_map/ppermute | solution.py:19
  75.8 1.9 collective-permute-start.1
  77.9 5.0 %collective-permute-start.8 = (bf16[512,128]{1,0:T(8,128)(2,1)}, bf16[512,128]{1,0:T(8,128)(2,1)}, u32[]{:S(2)}, u32[]{:S(2)}) collective-permute-start(bf16[512,128]{1,0:T(8,128)(2,1)} %bitcast.50), channel_id=1, source_target_pairs={{0,1},{1,2},{2,3},{3,4},{4,5},{5,6},{6,7},{8,9},{9,10},{10,11},{11... | collective-permute-start | bytes 393224 | tf_op jit(solution)/shard_map/ppermute | solution.py:31
  82.9 2.4 %slice_multiply_fusion.31 = f32[542,256]{1,0:T(8,128)S(1)} fusion(f32[572,256]{1,0:T(8,128)S(1)} %maximum_convert_fusion, f32[572,256]{1,0:T(8,128)S(1)} %maximum_convert_fusion.1, f32[256]{0:T(256)S(1)} %bitcast.221, f32[256]{0:T(256)S(1)} %bitcast.223, f32[256]{0:T(256)S(1)} %bitcast.225, f32[256]{0:T(256)S(1)} %bitcast.227, f32[256]{0:T(256)S(1)} %bitcast.229, ...), kind=kLoop, calls=%fused_computation.140 | loop fusion | flops 9573888 | bytes 18347008 | tf_op jit(solution)/shard_map/mul | solution.py:46
  85.4 2.8 %fusion.71 = bf16[512,256]{1,0:T(8,128)(2,1)} fusion(f32[542,256]{1,0:T(8,128)S(1)} %slice_multiply_fusion.31, f32[572,256]{1,0:T(8,128)S(1)} %maximum_convert_fusion, f32[256]{0:T(256)S(1)} %bitcast.222, f32[256]{0:T(256)S(1)} %bitcast.224, f32[256]{0:T(256)S(1)} %bitcast.226, f32[256]{0:T(256)S(1)} %bitcast.228, f32[256]{0:T(256)S(1)} %bitcast.230, ...), kind=kLoop, calls=%fused_computation.143 | loop fusion | flops 8257536 | bytes 17071104 | tf_op jit(solution)/shard_map/convert_element_type | solution.py:51
  88.2 1.6 fusion.115
  91.0 1.9 collective-permute-start.7
  92.9 1.7 copy.123
  94.6 4.9 %collective-permute-start.5 = (bf16[512,128]{1,0:T(8,128)(2,1)}, bf16[512,128]{1,0:T(8,128)(2,1)}, u32[]{:S(2)}, u32[]{:S(2)}) collective-permute-start(bf16[512,128]{1,0:T(8,128)(2,1)} %collective-permute-done.4), channel_id=1, source_target_pairs={{0,1},{1,2},{2,3},{3,4},{4,5},{5,6},{6,7},{8,9},{9,10},{10,11},{11... | collective-permute-start | bytes 393224 | tf_op jit(solution)/shard_map/ppermute | solution.py:31
  99.6 1.9 collective-permute-start.11
  101.5 4.8 %collective-permute-start.9 = (bf16[512,128]{1,0:T(8,128)(2,1)}, bf16[512,128]{1,0:T(8,128)(2,1)}, u32[]{:S(2)}, u32[]{:S(2)}) collective-permute-start(bf16[512,128]{1,0:T(8,128)(2,1)} %collective-permute-done.8), channel_id=1, source_target_pairs={{0,1},{1,2},{2,3},{3,4},{4,5},{5,6},{6,7},{8,9},{9,10},{10,11},{11... | collective-permute-start | bytes 393224 | tf_op jit(solution)/shard_map/ppermute | solution.py:31
  106.4 3.5 %fusion.113 = (f32[2,512]{1,0:T(2,128)}, f32[2,512,512]{1,2,0:T(8,128)}) fusion(bf16[512,2,64]{0,2,1:T(8,128)(2,1)S(1)} %reshape_squeeze.12, bf16[512,2,64]{0,2,1:T(8,128)(2,1)S(1)} %bitcast.213, pred[512,512]{0,1:T(8,128)(4,1)} %get-tuple-element.78), kind=kOutput, calls=%fused_computation.237 | convolution fusion | flops 68680704 | bytes 2625536 | tf_op jit(solution)/shard_map/qhd,khd->hqk/dot_general | solution.py:125
  109.9 2.5 %fusion.114 = (f32[2,512]{1,0:T(2,128)}, f32[2,512,512]{1,2,0:T(8,128)}) fusion(bf16[512,2,64]{0,2,1:T(8,128)(2,1)S(1)} %reshape_squeeze.12, bf16[512,2,64]{0,2,1:T(8,128)(2,1)S(1)} %bitcast.217, pred[512,512]{0,1:T(8,128)(4,1)S(1)} %copy-done.27), kind=kOutput, calls=%fused_computation.238 | convolution fusion | flops 68680704 | bytes 2625536 | tf_op jit(solution)/shard_map/qhd,khd->hqk/dot_general | solution.py:125
  112.4 1.7 copy.131
  114.0 1.7 copy.130
  116.7 1.7 copy.122
  118.4 1.7 copy.132
  120.1 1.7 copy.129
  121.8 3.0 %fusion.116 = (f32[2,512]{1,0:T(2,128)S(1)}, f32[2,512,512]{1,2,0:T(8,128)}) fusion(bf16[512,2,64]{0,2,1:T(8,128)(2,1)S(1)} %reshape_squeeze.12, bf16[512,2,64]{0,2,1:T(8,128)(2,1)} %bitcast.215, pred[512,512]{0,1:T(8,128)(4,1)} %get-tuple-element.76), kind=kOutput, calls=%fused_computation.240 | convolution fusion | flops 68680704 | bytes 2625536 | tf_op jit(solution)/shard_map/qhd,khd->hqk/dot_general | solution.py:125
  124.8 2.0 fusion.112
  126.9 1.7 convolution_convert_fusion.5
  136.1 1.1 convolution_convert_fusion.2
  138.4 1.1 convolution_convert_fusion
  139.5 1.2 fusion.12
  140.7 4.3 %multiply_convert_fusion = (bf16[2,512,512]{1,2,0:T(8,128)(2,1)}, bf16[2,512,512]{1,2,0:T(8,128)(2,1)}, bf16[2,512,512]{1,2,0:T(8,128)(2,1)}, bf16[2,512,512]{1,2,0:T(8,128)(2,1)S(1)}, bf16[2,512,512]{1,2,0:T(8,128)(2,1)}) fusion(f32[2,512,512]{1,2,0:T(8,128)S(1)} %get-tuple-element.96, f32[2,512,512]{1,2,0:T(8,128)S(1)} %copy-done.4, ...), kind=kLoop, calls=%fused_computation | loop fusion | flops 10485760 | bytes 26222592 | tf_op jit(solution)/shard_map/convert_element_type | solution.py:159
  151.5 1.7 copy.147
  153.2 2.3 %fusion.15 = bf16[2,512,64]{1,2,0:T(8,128)(2,1)} fusion(bf16[2,512,512]{1,2,0:T(8,128)(2,1)} %get-tuple-element.72, bf16[512,2,64]{0,2,1:T(8,128)(2,1)S(1)} %reshape_squeeze.12), kind=kOutput, calls=%fused_computation.54 | convolution fusion | flops 67239936 | bytes 1310720 | tf_op jit(solution)/shard_map/hqk,qhd->khd/dot_general | solution.py:168
  155.5 1.7 copy.140
  157.2 2.3 %fusion.16 = bf16[2,512,64]{1,2,0:T(8,128)(2,1)} fusion(bf16[2,512,512]{1,2,0:T(8,128)(2,1)} %get-tuple-element.73, bf16[512,2,64]{0,2,1:T(8,128)(2,1)S(1)} %reshape_squeeze.12), kind=kOutput, calls=%fused_computation.55 | convolution fusion | flops 67239936 | bytes 1310720 | tf_op jit(solution)/shard_map/hqk,qhd->khd/dot_general | solution.py:168
  159.5 1.6 copy.143
  161.1 1.7 copy.145
  162.8 1.3 fusion.117
  164.1 1.6 convolution_add_fusion.2
  167.1 1.7 copy.158
  168.7 2.0 collective-permute-start.14
  170.8 3.8 %collective-permute-start.13 = (bf16[512,128]{1,0:T(8,128)(2,1)}, bf16[512,128]{1,0:T(8,128)(2,1)S(1)}, u32[]{:S(2)}, u32[]{:S(2)}) collective-permute-start(bf16[512,128]{1,0:T(8,128)(2,1)} %copy.143), channel_id=1, source_target_pairs={{1,0},{2,1},{3,2},{4,3},{5,4},{6,5},{7,6},{9,8},{10,9},{11,10},{12... | collective-permute-start | bytes 393224 | tf_op jit(solution)/shard_map/ppermute | solution.py:31
  174.6 2.4 %collective-permute-start.12 = (bf16[512,128]{1,0:T(8,128)(2,1)}, bf16[512,128]{1,0:T(8,128)(2,1)S(1)}, u32[]{:S(2)}, u32[]{:S(2)}) collective-permute-start(bf16[512,128]{1,0:T(8,128)(2,1)} %copy.140), channel_id=1, source_target_pairs={{2,0},{3,1},{4,2},{5,3},{6,4},{7,5},{10,8},{11,9},{12,10},{13,11},... | collective-permute-start | bytes 393224 | tf_op jit(solution)/shard_map/ppermute | solution.py:31
  177.0 3.5 %collective-permute-start.15 = (bf16[512,128]{1,0:T(8,128)(2,1)}, bf16[512,128]{1,0:T(8,128)(2,1)S(1)}, u32[]{:S(2)}, u32[]{:S(2)}) collective-permute-start(bf16[512,128]{1,0:T(8,128)(2,1)} %copy.147), channel_id=1, source_target_pairs={{0,2},{1,3},{2,4},{3,5},{4,6},{5,7},{8,10},{9,11},{10,12},{11,13},... | collective-permute-start | bytes 393224 | tf_op jit(solution)/shard_map/ppermute | solution.py:31
  181.0 2.4 %collective-permute-start.16 = (bf16[512,128]{1,0:T(8,128)(2,1)}, bf16[512,128]{1,0:T(8,128)(2,1)S(1)}, u32[]{:S(2)}, u32[]{:S(2)}) collective-permute-start(bf16[512,128]{1,0:T(8,128)(2,1)} %copy.150), channel_id=1, source_target_pairs={{2,0},{3,1},{4,2},{5,3},{6,4},{7,5},{10,8},{11,9},{12,10},{13,11},... | collective-permute-start | bytes 393224 | tf_op jit(solution)/shard_map/ppermute | solution.py:31
  183.4 1.9 collective-permute-start.17
  185.3 4.8 %collective-permute-start.18 = (bf16[512,128]{1,0:T(8,128)(2,1)}, bf16[512,128]{1,0:T(8,128)(2,1)S(1)}, u32[]{:S(2)}, u32[]{:S(2)}) collective-permute-start(bf16[512,128]{1,0:T(8,128)(2,1)} %copy.155), channel_id=1, source_target_pairs={{0,1},{1,2},{2,3},{3,4},{4,5},{5,6},{6,7},{8,9},{9,10},{10,11},{11... | collective-permute-start | bytes 393224 | tf_op jit(solution)/shard_map/ppermute | solution.py:31
  190.2 3.5 %collective-permute-start.19 = (bf16[512,128]{1,0:T(8,128)(2,1)}, bf16[512,128]{1,0:T(8,128)(2,1)S(1)}, u32[]{:S(2)}, u32[]{:S(2)}) collective-permute-start(bf16[512,128]{1,0:T(8,128)(2,1)} %copy.157), channel_id=1, source_target_pairs={{0,2},{1,3},{2,4},{3,5},{4,6},{5,7},{8,10},{9,11},{10,12},{11,13},... | collective-permute-start | bytes 393224 | tf_op jit(solution)/shard_map/ppermute | solution.py:31
  194.4 2.8 %collective-permute-done.19 = bf16[512,128]{1,0:T(8,128)(2,1)S(1)} collective-permute-done((bf16[512,128]{1,0:T(8,128)(2,1)}, bf16[512,128]{1,0:T(8,128)(2,1)S(1)}, u32[]{:S(2)}, u32[]{:S(2)}) %collective-permute-start.19) | collective-permute-done | bytes 131104 | tf_op jit(solution)/shard_map/ppermute | solution.py:31
  (161 shorter events, 30.7 us)
Async XLA Ops:
  7.2 119.7 %copy-start = (bf16[512,1024]{1,0:T(8,128)(2,1)S(1)}, bf16[512,1024]{1,0:T(8,128)(2,1)}, u32[]{:S(2)}) copy-start(bf16[512,1024]{1,0:T(8,128)(2,1)} %param.13) | copy-start | bytes 3145732
  7.2 15.4 %copy-start.28 = (bf16[1,128,512]{2,1,0:T(8,128)(2,1)S(1)}, bf16[1,128,512]{2,1,0:T(8,128)(2,1)}, u32[]{:S(2)}) copy-start(bf16[1,128,512]{2,1,0:T(8,128)(2,1)} %param.9) | copy-start | bytes 393220
  7.2 17.7 %copy-start.29 = (bf16[1,128,512]{2,1,0:T(8,128)(2,1)S(1)}, bf16[1,128,512]{2,1,0:T(8,128)(2,1)}, u32[]{:S(2)}) copy-start(bf16[1,128,512]{2,1,0:T(8,128)(2,1)} %param.10) | copy-start | bytes 393220
  11.0 16.2 %all-to-all-start.2 = ((bf16[4,2,8192]{2,1,0:T(2,128)(2,1)}), bf16[4,2,8192]{2,1,0:T(2,128)(2,1)S(1)}, u32[]{:S(2)}, u32[]{:S(2)}) async-start(bf16[4,2,8192]{2,1,0:T(2,128)(2,1)} %reshape.507), calls=%async_computation.2 | async-start | bytes 262144 | tf_op jit(solution)/shard_map/all_to_all | solution.py:59
  14.8 23.7 %copy-start.24 = (bf16[1,128,1024]{2,1,0:T(8,128)(2,1)S(1)}, bf16[1,128,1024]{2,1,0:T(8,128)(2,1)}, u32[]{:S(2)}) copy-start(bf16[1,128,1024]{2,1,0:T(8,128)(2,1)} %param.11) | copy-start | bytes 786436
  24.2 17.7 %copy-start.25 = (bf16[1,128,1024]{2,1,0:T(8,128)(2,1)S(1)}, bf16[1,128,1024]{2,1,0:T(8,128)(2,1)}, u32[]{:S(2)}) copy-start(bf16[1,128,1024]{2,1,0:T(8,128)(2,1)} %param.12) | copy-start | bytes 786436
  27.2 6.4 %all-to-all-start.3 = ((bf16[4,2,8192]{2,1,0:T(2,128)(2,1)}), bf16[4,2,8192]{2,1,0:T(2,128)(2,1)S(1)}, u32[]{:S(2)}, u32[]{:S(2)}) async-start(bf16[4,2,8192]{2,1,0:T(2,128)(2,1)} %reshape.503), calls=%async_computation.3 | async-start | bytes 262144 | tf_op jit(solution)/shard_map/all_to_all | solution.py:60
  33.5 11.8 %all-to-all-start.4 = ((bf16[4,2,8192]{2,1,0:T(2,128)(2,1)}), bf16[4,2,8192]{2,1,0:T(2,128)(2,1)S(1)}, u32[]{:S(2)}, u32[]{:S(2)}) async-start(bf16[4,2,8192]{2,1,0:T(2,128)(2,1)} %reshape.505), calls=%async_computation.4 | async-start | bytes 262144 | tf_op jit(solution)/shard_map/all_to_all | solution.py:61
  45.3 14.5 %all-to-all-start.1 = ((bf16[4,2,16384]{2,1,0:T(2,128)(2,1)}), bf16[4,2,16384]{2,1,0:T(2,128)(2,1)S(1)}, u32[]{:S(2)}, u32[]{:S(2)}) async-start(bf16[4,2,16384]{2,1,0:T(2,128)(2,1)} %reshape.501), calls=%async_computation.1 | async-start | bytes 524288 | tf_op jit(solution)/shard_map/all_to_all | solution.py:62
  49.7 40.2 %collective-permute-start.6 = (bf16[512,128]{1,0:T(8,128)(2,1)}, bf16[512,128]{1,0:T(8,128)(2,1)}, u32[]{:S(2)}, u32[]{:S(2)}) collective-permute-start(bf16[512,128]{1,0:T(8,128)(2,1)} %bitcast.40), channel_id=1, source_target_pairs={{1,0},{2,1},{3,2},{4,3},{5,4},{6,5},{7,6},{9,8},{10,9},{11,10},{12... | collective-permute-start | bytes 393224 | tf_op jit(solution)/shard_map/ppermute | solution.py:31
  52.2 40.8 %collective-permute-start.4 = (bf16[512,128]{1,0:T(8,128)(2,1)}, bf16[512,128]{1,0:T(8,128)(2,1)}, u32[]{:S(2)}, u32[]{:S(2)}) collective-permute-start(bf16[512,128]{1,0:T(8,128)(2,1)} %bitcast.40), channel_id=1, source_target_pairs={{0,1},{1,2},{2,3},{3,4},{4,5},{5,6},{6,7},{8,9},{9,10},{10,11},{11... | collective-permute-start | bytes 393224 | tf_op jit(solution)/shard_map/ppermute | solution.py:31
  56.9 31.3 %copy-start.19 = (bf16[512,2,64]{0,2,1:T(8,128)(2,1)}, bf16[512,2,64]{0,2,1:T(8,128)(2,1)S(1)}, u32[]{:S(2)}) copy-start(bf16[512,2,64]{0,2,1:T(8,128)(2,1)S(1)} %reshape_squeeze.13) | copy-start | bytes 393220
  57.8 41.7 %collective-permute-start.10 = (bf16[512,128]{1,0:T(8,128)(2,1)}, bf16[512,128]{1,0:T(8,128)(2,1)}, u32[]{:S(2)}, u32[]{:S(2)}) collective-permute-start(bf16[512,128]{1,0:T(8,128)(2,1)} %bitcast.50), channel_id=1, source_target_pairs={{1,0},{2,1},{3,2},{4,3},{5,4},{6,5},{7,6},{9,8},{10,9},{11,10},{12... | collective-permute-start | bytes 393224 | tf_op jit(solution)/shard_map/ppermute | solution.py:31
  59.8 10.7 %all-to-all-start = ((bf16[4,2,16384]{2,1,0:T(2,128)(2,1)}), bf16[4,2,16384]{2,1,0:T(2,128)(2,1)S(1)}, u32[]{:S(2)}, u32[]{:S(2)}) async-start(bf16[4,2,16384]{2,1,0:T(2,128)(2,1)} %reshape.499), calls=%async_computation | async-start | bytes 524288 | tf_op jit(solution)/shard_map/all_to_all | solution.py:63
  63.2 63.7 %all-gather.2.cloned.1.call-start = ((), (), s32[]{:S(2)}) async-start(), calls=%async_computation.5 | async-start | bytes 1310720 | tf_op jit(solution)/shard_map/all_gather | solution.py:85
  63.7 7.3 %collective-permute-start.2 = (bf16[30,256]{1,0:T(8,128)(2,1)S(1)}, bf16[30,256]{1,0:T(8,128)(2,1)S(1)}, u32[]{:S(2)}, u32[]{:S(2)}) collective-permute-start(bf16[30,256]{1,0:T(8,128)(2,1)S(1)} %get-tuple-element.36), channel_id=1, source_target_pairs={{0,1},{1,2},{2,3},{3,4},{4,5},{5,6},{6,7},{8,9},{9,10},{10,11},{11... | collective-permute-start | bytes 46088 | tf_op jit(solution)/shard_map/ppermute | solution.py:19
  68.6 7.3 %collective-permute-start.3 = (bf16[30,256]{1,0:T(8,128)(2,1)S(1)}, bf16[30,256]{1,0:T(8,128)(2,1)S(1)}, u32[]{:S(2)}, u32[]{:S(2)}) collective-permute-start(bf16[30,256]{1,0:T(8,128)(2,1)S(1)} %get-tuple-element.37), channel_id=1, source_target_pairs={{1,0},{2,1},{3,2},{4,3},{5,4},{6,5},{7,6},{9,8},{10,9},{11,10},{12... | collective-permute-start | bytes 46088 | tf_op jit(solution)/shard_map/ppermute | solution.py:21
  71.0 6.8 %collective-permute-start = (bf16[30,256]{1,0:T(8,128)(2,1)S(1)}, bf16[30,256]{1,0:T(8,128)(2,1)S(1)}, u32[]{:S(2)}, u32[]{:S(2)}) collective-permute-start(bf16[30,256]{1,0:T(8,128)(2,1)S(1)} %get-tuple-element.38), channel_id=1, source_target_pairs={{0,1},{1,2},{2,3},{3,4},{4,5},{5,6},{6,7},{8,9},{9,10},{10,11},{11... | collective-permute-start | bytes 46088 | tf_op jit(solution)/shard_map/ppermute | solution.py:19
  75.8 7.0 %collective-permute-start.1 = (bf16[30,256]{1,0:T(8,128)(2,1)S(1)}, bf16[30,256]{1,0:T(8,128)(2,1)S(1)}, u32[]{:S(2)}, u32[]{:S(2)}) collective-permute-start(bf16[30,256]{1,0:T(8,128)(2,1)S(1)} %get-tuple-element.39), channel_id=1, source_target_pairs={{1,0},{2,1},{3,2},{4,3},{5,4},{6,5},{7,6},{9,8},{10,9},{11,10},{12... | collective-permute-start | bytes 46088 | tf_op jit(solution)/shard_map/ppermute | solution.py:21
  77.9 23.7 %collective-permute-start.8 = (bf16[512,128]{1,0:T(8,128)(2,1)}, bf16[512,128]{1,0:T(8,128)(2,1)}, u32[]{:S(2)}, u32[]{:S(2)}) collective-permute-start(bf16[512,128]{1,0:T(8,128)(2,1)} %bitcast.50), channel_id=1, source_target_pairs={{0,1},{1,2},{2,3},{3,4},{4,5},{5,6},{6,7},{8,9},{9,10},{10,11},{11... | collective-permute-start | bytes 393224 | tf_op jit(solution)/shard_map/ppermute | solution.py:31
  91.0 21.4 %copy-start.20 = (bf16[512,128]{0,1:T(8,128)(2,1)}, bf16[512,128]{0,1:T(8,128)(2,1)S(1)}, u32[]{:S(2)}) copy-start(bf16[512,128]{0,1:T(8,128)(2,1)S(1)} %copy.124) | copy-start | bytes 393220
  91.0 24.7 %collective-permute-start.7 = (bf16[512,128]{1,0:T(8,128)(2,1)}, bf16[512,128]{1,0:T(8,128)(2,1)}, u32[]{:S(2)}, u32[]{:S(2)}) collective-permute-start(bf16[512,128]{1,0:T(8,128)(2,1)} %collective-permute-done.6), channel_id=1, source_target_pairs={{1,0},{2,1},{3,2},{4,3},{5,4},{6,5},{7,6},{9,8},{10,9},{11,10},{12... | collective-permute-start | bytes 393224 | tf_op jit(solution)/shard_map/ppermute | solution.py:31
  94.6 15.2 %copy-start.22 = (bf16[512,128]{0,1:T(8,128)(2,1)S(1)}, bf16[512,128]{0,1:T(8,128)(2,1)}, u32[]{:S(2)}) copy-start(bf16[512,128]{0,1:T(8,128)(2,1)} %copy.123) | copy-start | bytes 393220
  94.6 15.2 %copy-start.27 = (pred[512,512]{0,1:T(8,128)(4,1)S(1)}, pred[512,512]{0,1:T(8,128)(4,1)}, u32[]{:S(2)}) copy-start(pred[512,512]{0,1:T(8,128)(4,1)} %get-tuple-element.77) | copy-start | bytes 786436
  94.6 22.1 %collective-permute-start.5 = (bf16[512,128]{1,0:T(8,128)(2,1)}, bf16[512,128]{1,0:T(8,128)(2,1)}, u32[]{:S(2)}, u32[]{:S(2)}) collective-permute-start(bf16[512,128]{1,0:T(8,128)(2,1)} %collective-permute-done.4), channel_id=1, source_target_pairs={{0,1},{1,2},{2,3},{3,4},{4,5},{5,6},{6,7},{8,9},{9,10},{10,11},{11... | collective-permute-start | bytes 393224 | tf_op jit(solution)/shard_map/ppermute | solution.py:31
  99.6 18.9 %collective-permute-start.11 = (bf16[512,128]{1,0:T(8,128)(2,1)}, bf16[512,128]{1,0:T(8,128)(2,1)}, u32[]{:S(2)}, u32[]{:S(2)}) collective-permute-start(bf16[512,128]{1,0:T(8,128)(2,1)} %collective-permute-done.10), channel_id=1, source_target_pairs={{1,0},{2,1},{3,2},{4,3},{5,4},{6,5},{7,6},{9,8},{10,9},{11,10},{12... | collective-permute-start | bytes 393224 | tf_op jit(solution)/shard_map/ppermute | solution.py:31
  101.5 18.6 %collective-permute-start.9 = (bf16[512,128]{1,0:T(8,128)(2,1)}, bf16[512,128]{1,0:T(8,128)(2,1)}, u32[]{:S(2)}, u32[]{:S(2)}) collective-permute-start(bf16[512,128]{1,0:T(8,128)(2,1)} %collective-permute-done.8), channel_id=1, source_target_pairs={{0,1},{1,2},{2,3},{3,4},{4,5},{5,6},{6,7},{8,9},{9,10},{10,11},{11... | collective-permute-start | bytes 393224 | tf_op jit(solution)/shard_map/ppermute | solution.py:31
  116.7 10.1 %copy-start.10 = (bf16[512,128]{0,1:T(8,128)(2,1)}, bf16[512,128]{0,1:T(8,128)(2,1)S(1)}, u32[]{:S(2)}) copy-start(bf16[512,128]{0,1:T(8,128)(2,1)S(1)} %copy.125) | copy-start | bytes 393220
  121.8 3.0 %copy-start.26 = (pred[512,512]{0,1:T(8,128)(4,1)S(1)}, pred[512,512]{0,1:T(8,128)(4,1)}, u32[]{:S(2)}) copy-start(pred[512,512]{0,1:T(8,128)(4,1)} %get-tuple-element.79) | copy-start | bytes 786436
  121.8 5.1 %copy-start.32 = (f32[2,512]{1,0:T(2,128)S(1)}, f32[2,512]{1,0:T(2,128)}, u32[]{:S(2)}) copy-start(f32[2,512]{1,0:T(2,128)} %get-tuple-element.88) | copy-start | bytes 12292
  121.8 5.1 %copy-start.33 = (f32[2,512]{1,0:T(2,128)S(1)}, f32[2,512]{1,0:T(2,128)}, u32[]{:S(2)}) copy-start(f32[2,512]{1,0:T(2,128)} %get-tuple-element.90) | copy-start | bytes 12292
  126.9 8.8 %copy-start.30 = (f32[2,512]{1,0:T(2,128)}, f32[2,512]{1,0:T(2,128)S(1)}, u32[]{:S(2)}) copy-start(f32[2,512]{1,0:T(2,128)S(1)} %get-tuple-element.35) | copy-start | bytes 12292
  128.6 1.6 copy-start.4
  128.6 1.6 copy-start.18
  130.2 1.6 copy-start.1
  130.2 1.6 copy-start.13
  131.8 1.6 copy-start.2
  131.8 1.6 copy-start.12
  133.4 1.6 copy-start.3
  133.4 1.6 copy-start.14
  138.4 2.3 %copy-start.31 = (f32[2,512]{1,0:T(2,128)S(1)}, f32[2,512]{1,0:T(2,128)}, u32[]{:S(2)}) copy-start(f32[2,512]{1,0:T(2,128)} %copy-done.30) | copy-start | bytes 12292
  140.7 5.4 %copy-start.21 = (bf16[512,128]{0,1:T(8,128)(2,1)S(1)}, bf16[512,128]{0,1:T(8,128)(2,1)}, u32[]{:S(2)}) copy-start(bf16[512,128]{0,1:T(8,128)(2,1)} %copy-done.20) | copy-start | bytes 393220
  145.0 2.2 %copy-start.8 = (f32[2,64,512]{2,1,0:T(8,128)S(1)}, f32[2,64,512]{2,1,0:T(8,128)}, u32[]{:S(2)}) copy-start(f32[2,64,512]{2,1,0:T(8,128)} %fusion.12) | copy-start | bytes 786436
  145.0 2.3 %copy-start.17 = (bf16[2,64,512]{2,1,0:T(8,128)(2,1)S(1)}, bf16[2,64,512]{2,1,0:T(8,128)(2,1)}, u32[]{:S(2)}) copy-start(bf16[2,64,512]{2,1,0:T(8,128)(2,1)} %convolution_convert_fusion) | copy-start | bytes 393220
  145.0 3.1 %copy-start.16 = (bf16[2,64,512]{2,1,0:T(8,128)(2,1)S(1)}, bf16[2,64,512]{2,1,0:T(8,128)(2,1)}, u32[]{:S(2)}) copy-start(bf16[2,64,512]{2,1,0:T(8,128)(2,1)} %convolution_convert_fusion.1) | copy-start | bytes 393220
  145.0 3.8 %copy-start.15 = (bf16[2,64,512]{2,1,0:T(8,128)(2,1)S(1)}, bf16[2,64,512]{2,1,0:T(8,128)(2,1)}, u32[]{:S(2)}) copy-start(bf16[2,64,512]{2,1,0:T(8,128)(2,1)} %convolution_convert_fusion.2) | copy-start | bytes 393220
  145.0 5.4 %copy-start.6 = (bf16[2,512,512]{1,2,0:T(8,128)(2,1)S(1)}, bf16[2,512,512]{1,2,0:T(8,128)(2,1)}, u32[]{:S(2)}) copy-start(bf16[2,512,512]{1,2,0:T(8,128)(2,1)} %get-tuple-element.71) | copy-start | bytes 3145732
  151.5 11.4 %copy-start.5 = (bf16[2,512,512]{1,2,0:T(8,128)(2,1)S(1)}, bf16[2,512,512]{1,2,0:T(8,128)(2,1)}, u32[]{:S(2)}) copy-start(bf16[2,512,512]{1,2,0:T(8,128)(2,1)} %get-tuple-element.75) | copy-start | bytes 3145732
  162.8 3.0 %copy-start.7 = (bf16[2,512,512]{1,2,0:T(8,128)(2,1)S(1)}, bf16[2,512,512]{1,2,0:T(8,128)(2,1)}, u32[]{:S(2)}) copy-start(bf16[2,512,512]{1,2,0:T(8,128)(2,1)} %get-tuple-element.73) | copy-start | bytes 3145732
  162.8 3.0 %copy-start.9 = (f32[2,512,64]{1,2,0:T(8,128)S(1)}, f32[2,512,64]{1,2,0:T(8,128)}, u32[]{:S(2)}) copy-start(f32[2,512,64]{1,2,0:T(8,128)} %fusion.118) | copy-start | bytes 786436
  162.8 3.0 %copy-start.23 = (bf16[512,128]{0,1:T(8,128)(2,1)S(1)}, bf16[512,128]{0,1:T(8,128)(2,1)}, u32[]{:S(2)}) copy-start(bf16[512,128]{0,1:T(8,128)(2,1)} %copy.123) | copy-start | bytes 393220
  164.1 2.0 copy-start.11
  168.7 14.6 %collective-permute-start.14 = (bf16[512,128]{1,0:T(8,128)(2,1)}, bf16[512,128]{1,0:T(8,128)(2,1)S(1)}, u32[]{:S(2)}, u32[]{:S(2)}) collective-permute-start(bf16[512,128]{1,0:T(8,128)(2,1)} %copy.145), channel_id=1, source_target_pairs={{0,1},{1,2},{2,3},{3,4},{4,5},{5,6},{6,7},{8,9},{9,10},{10,11},{11... | collective-permute-start | bytes 393224 | tf_op jit(solution)/shard_map/ppermute | solution.py:31
  170.8 14.6 %collective-permute-start.13 = (bf16[512,128]{1,0:T(8,128)(2,1)}, bf16[512,128]{1,0:T(8,128)(2,1)S(1)}, u32[]{:S(2)}, u32[]{:S(2)}) collective-permute-start(bf16[512,128]{1,0:T(8,128)(2,1)} %copy.143), channel_id=1, source_target_pairs={{1,0},{2,1},{3,2},{4,3},{5,4},{6,5},{7,6},{9,8},{10,9},{11,10},{12... | collective-permute-start | bytes 393224 | tf_op jit(solution)/shard_map/ppermute | solution.py:31
  174.6 15.6 %collective-permute-start.12 = (bf16[512,128]{1,0:T(8,128)(2,1)}, bf16[512,128]{1,0:T(8,128)(2,1)S(1)}, u32[]{:S(2)}, u32[]{:S(2)}) collective-permute-start(bf16[512,128]{1,0:T(8,128)(2,1)} %copy.140), channel_id=1, source_target_pairs={{2,0},{3,1},{4,2},{5,3},{6,4},{7,5},{10,8},{11,9},{12,10},{13,11},... | collective-permute-start | bytes 393224 | tf_op jit(solution)/shard_map/ppermute | solution.py:31
  177.0 16.7 %collective-permute-start.15 = (bf16[512,128]{1,0:T(8,128)(2,1)}, bf16[512,128]{1,0:T(8,128)(2,1)S(1)}, u32[]{:S(2)}, u32[]{:S(2)}) collective-permute-start(bf16[512,128]{1,0:T(8,128)(2,1)} %copy.147), channel_id=1, source_target_pairs={{0,2},{1,3},{2,4},{3,5},{4,6},{5,7},{8,10},{9,11},{10,12},{11,13},... | collective-permute-start | bytes 393224 | tf_op jit(solution)/shard_map/ppermute | solution.py:31
  181.0 13.4 %collective-permute-start.16 = (bf16[512,128]{1,0:T(8,128)(2,1)}, bf16[512,128]{1,0:T(8,128)(2,1)S(1)}, u32[]{:S(2)}, u32[]{:S(2)}) collective-permute-start(bf16[512,128]{1,0:T(8,128)(2,1)} %copy.150), channel_id=1, source_target_pairs={{2,0},{3,1},{4,2},{5,3},{6,4},{7,5},{10,8},{11,9},{12,10},{13,11},... | collective-permute-start | bytes 393224 | tf_op jit(solution)/shard_map/ppermute | solution.py:31
  183.4 11.0 %collective-permute-start.17 = (bf16[512,128]{1,0:T(8,128)(2,1)}, bf16[512,128]{1,0:T(8,128)(2,1)S(1)}, u32[]{:S(2)}, u32[]{:S(2)}) collective-permute-start(bf16[512,128]{1,0:T(8,128)(2,1)} %copy.153), channel_id=1, source_target_pairs={{1,0},{2,1},{3,2},{4,3},{5,4},{6,5},{7,6},{9,8},{10,9},{11,10},{12... | collective-permute-start | bytes 393224 | tf_op jit(solution)/shard_map/ppermute | solution.py:31
  185.3 9.1 %collective-permute-start.18 = (bf16[512,128]{1,0:T(8,128)(2,1)}, bf16[512,128]{1,0:T(8,128)(2,1)S(1)}, u32[]{:S(2)}, u32[]{:S(2)}) collective-permute-start(bf16[512,128]{1,0:T(8,128)(2,1)} %copy.155), channel_id=1, source_target_pairs={{0,1},{1,2},{2,3},{3,4},{4,5},{5,6},{6,7},{8,9},{9,10},{10,11},{11... | collective-permute-start | bytes 393224 | tf_op jit(solution)/shard_map/ppermute | solution.py:31
  190.2 7.1 %collective-permute-start.19 = (bf16[512,128]{1,0:T(8,128)(2,1)}, bf16[512,128]{1,0:T(8,128)(2,1)S(1)}, u32[]{:S(2)}, u32[]{:S(2)}) collective-permute-start(bf16[512,128]{1,0:T(8,128)(2,1)} %copy.157), channel_id=1, source_target_pairs={{0,2},{1,3},{2,4},{3,5},{4,6},{5,7},{8,10},{9,11},{10,12},{11,13},... | collective-permute-start | bytes 393224 | tf_op jit(solution)/shard_map/ppermute | solution.py:31
Sparse Core Ops, SparseCore 0:
  88.3 15.9 all-gather.1
where the time goes:
time: 207 us; the launch traced here: 205 us
  starting transfers between devices  84.1 us (41%)
  local copies, waits for them, and re-layouts  39.1 us (19%)
  matrix products  34.8 us (17%)
  other arithmetic  26.7 us (13%)
  between operations  14.9 us (7%)
  waiting for transfers between devices  5.17 us (2%)
    ppermute x16, starting transfers between devices, shifted(): lax.ppermute(value, axis, [(source, source + steps) for source in range(f...  51.5 us
    unnamed x90, local copies, waits for them, and re-layouts  13.2 us
    dot_general x5, matrix products, block_logits(): jnp.einsum('qhd,khd->hqk', query_heads, keys_now, preferred_element_type=...  12.6 us
    ppermute x8, local copies, waits for them, and re-layouts, shifted(): lax.ppermute(value, axis, [(source, source + steps) for source in range(f...  12 us
    ppermute x2, starting transfers between devices, padded(): lax.ppermute(tail, axis, [(i, (i + 1) % count) for i in range(ends)])  9.64 us
    unnamed x5, other arithmetic  8.65 us
    dot_general x5, matrix products, on_device(): jnp.einsum('hqk,qhd->khd', dlogits, query_heads, preferred_element_type=j...  7.3 us
    reshape x4, local copies, waits for them, and re-layouts, on_device(): key_part = (jnp.einsum('hqk,qhd->khd', dlogits, query_heads, preferred_el...  6.71 us
  transfers between devices with their start and end apart: 26, of which 2 were waited for; matrix products, arithmetic and copies ran while one was open for 27% of the time, Pallas kernels for 0%

commit v1 on v0

--- a/solution.py
+++ b/solution.py
@@ -58,7 +58,10 @@
     moved = (
         lax.all_to_all(query, "head", split_axis=2, concat_axis=1, tiled=True),
         lax.all_to_all(key, "head", split_axis=2, concat_axis=1, tiled=True),
-        lax.all_to_all(value, "head", split_axis=2, concat_axis=1, tiled=True),
+        jnp.concatenate(
+            lax.all_to_all(jnp.stack(jnp.split(value, lax.axis_size("head"), 2), 0), "head", 0, 0),
+            1,
+        ),
         lax.all_to_all(resid_in, "head", split_axis=2, concat_axis=1, tiled=True),
         lax.all_to_all(out_grad, "head", split_axis=2, concat_axis=1, tiled=True),
     )

time: 207 us -> 200 us (0.966)
  local copies, waits for them, and re-layouts: 39.1 us -> 30 us
  matrix products: 34.8 us -> 38.3 us
    ppermute x8 -> x4, local copies, waits for them, and re-layouts: 12 us -> 5.4 us  [shifted(): lax.ppermute(value, axis, [(source, source + steps) for source in range(f...]
    unnamed x90 -> x72, local copies, waits for them, and re-layouts: 13.2 us -> 8.2 us
    dot_general x5, matrix products: 3 us -> 7.08 us  [block_slopes(): jnp.einsum('qhd,khd->hqk', grad_heads, values_now, preferred_element_type...]
    all_to_all x1, waiting for transfers between devices: 0.01 us -> 2.25 us  [on_device(): lax.all_to_all(query, 'head', split_axis=2, concat_axis=1, tiled=True)]
    all_to_all x1, waiting for transfers between devices: 2.25 us -> 0.01 us  [on_device(): lax.all_to_all(key, 'head', split_axis=2, concat_axis=1, tiled=True)]
    unnamed x5 -> x4, other arithmetic: 8.65 us -> 7.24 us
  transfers between devices with their start and end apart: 26 -> 26, of which waited for: 2 -> 2; matrix products, arithmetic and copies ran while one was open for 27% -> 28% of each run, Pallas kernels for 0% -> 0%
where the time goes in v1:
time: 200 us; the launch traced here: 198 us
  starting transfers between devices  84 us (42%)
  matrix products  38.3 us (19%)
  local copies, waits for them, and re-layouts  30 us (15%)
  other arithmetic  26 us (13%)
  between operations  14.9 us (7%)
  waiting for transfers between devices  5.18 us (3%)
    ppermute x16, starting transfers between devices, shifted(): lax.ppermute(value, axis, [(source, source + steps) for source in range(f...  51.5 us
    dot_general x5, matrix products, block_logits(): jnp.einsum('qhd,khd->hqk', query_heads, keys_now, preferred_element_type=...  11.4 us
    ppermute x2, starting transfers between devices, padded(): lax.ppermute(tail, axis, [(i, (i + 1) % count) for i in range(ends)])  9.64 us
    unnamed x72, local copies, waits for them, and re-layouts  8.2 us
    dot_general x5, matrix products, on_device(): jnp.einsum('hqk,qhd->khd', dlogits, query_heads, preferred_element_type=j...  7.27 us
    unnamed x4, other arithmetic  7.24 us
    dot_general x5, matrix products, block_slopes(): jnp.einsum('qhd,khd->hqk', grad_heads, values_now, preferred_element_type...  7.08 us
    reshape x4, local copies, waits for them, and re-layouts, on_device(): key_part = (jnp.einsum('hqk,qhd->khd', dlogits, query_heads, preferred_el...  6.73 us
  transfers between devices with their start and end apart: 26, of which 2 were waited for; matrix products, arithmetic and copies ran while one was open for 28% of the time, Pallas kernels for 0%

profile of v1, /device:TPU:14, one launch (start us, length us, event | category | flops | bytes accessed | tf_op | source)
XLA Modules:
  0.0 198.4 jit_solution(15439866209692085374)
XLA Ops:
  8.8 3.8 %all-to-all-start.4 = ((bf16[4,1,128,128]{3,2,1,0:T(8,128)(2,1)}), bf16[4,1,128,128]{3,2,1,0:T(8,128)(2,1)S(1)}, u32[]{:S(2)}, u32[]{:S(2)}) async-start(bf16[4,1,128,128]{3,2,1,0:T(8,128)(2,1)} %pad_maximum_fusion), calls=%async_computation.4 | async-start | bytes 262144 | tf_op jit(solution)/shard_map/all_to_all | solution.py:62
  12.6 1.5 fusion.111
  14.8 1.3 iota_compare_fusion.2
  16.1 1.4 iota_compare_fusion
  17.5 2.9 %fusion.33 = (pred[512,512]{0,1:T(8,128)(4,1)}, pred[512,512]{0,1:T(8,128)(4,1)}, pred[512,512]{0,1:T(8,128)(4,1)}, pred[512,512]{0,1:T(8,128)(4,1)}, pred[512,512]{0,1:T(8,128)(4,1)}) fusion(s32[512]{0:T(512)S(1)} %get-tuple-element.112, s32[512]{0:T(512)S(1)} %iota_add_fusion.4, pred[512]{0:T(512)(128)(4,1)S(1)} %get-tuple-element.110, pred[]{:T(512)S(6)} %and.169, ...), kind=kLoop, calls=%fused_computation.72 | loop fusion | flops 6553600 | bytes 1323525 | tf_op jit(solution)/shard_map/and | solution.py:113
  21.2 1.4 reduce.3
  23.5 1.4 reduce.2
  25.6 3.4 %all-to-all-start.2 = ((bf16[4,2,8192]{2,1,0:T(2,128)(2,1)}), bf16[4,2,8192]{2,1,0:T(2,128)(2,1)S(1)}, u32[]{:S(2)}, u32[]{:S(2)}) async-start(bf16[4,2,8192]{2,1,0:T(2,128)(2,1)} %reshape.503), calls=%async_computation.2 | async-start | bytes 262144 | tf_op jit(solution)/shard_map/all_to_all | solution.py:59
  29.7 2.2 %all-to-all-done.2 = bf16[4,2,8192]{2,1,0:T(2,128)(2,1)S(1)} async-done(((bf16[4,2,8192]{2,1,0:T(2,128)(2,1)}), bf16[4,2,8192]{2,1,0:T(2,128)(2,1)S(1)}, u32[]{:S(2)}, u32[]{:S(2)}) %all-to-all-start.2) | async-done | bytes 131104 | tf_op jit(solution)/shard_map/all_to_all | solution.py:59
  31.9 5.0 %all-to-all-start.3 = ((bf16[4,2,8192]{2,1,0:T(2,128)(2,1)}), bf16[4,2,8192]{2,1,0:T(2,128)(2,1)S(1)}, u32[]{:S(2)}, u32[]{:S(2)}) async-start(bf16[4,2,8192]{2,1,0:T(2,128)(2,1)} %reshape.501), calls=%async_computation.3 | async-start | bytes 262144 | tf_op jit(solution)/shard_map/all_to_all | solution.py:60
  37.3 2.2 %reduce.1 = bf16[1024,128]{1,0:T(8,128)(2,1)S(1)} reduce(bf16[1024,1,128]{2,1,0:T(2,128)(2,1)S(1)} %bitcast.180, bf16[]{:T(256)} %broadcast.279), dimensions={1}, to_apply=%bitcast.115.reduce_sub_computation | reduce | bytes 524290
  40.7 2.2 %reduce = bf16[1024,128]{1,0:T(8,128)(2,1)S(1)} reduce(bf16[1024,1,128]{2,1,0:T(2,128)(2,1)S(1)} %bitcast.179, bf16[]{:T(256)} %broadcast.279), dimensions={1}, to_apply=%bitcast.113.reduce_sub_computation | reduce | bytes 524290
  43.7 3.4 %all-to-all-start.1 = ((bf16[4,2,16384]{2,1,0:T(2,128)(2,1)}), bf16[4,2,16384]{2,1,0:T(2,128)(2,1)S(1)}, u32[]{:S(2)}, u32[]{:S(2)}) async-start(bf16[4,2,16384]{2,1,0:T(2,128)(2,1)} %reshape.499), calls=%async_computation.1 | async-start | bytes 524288 | tf_op jit(solution)/shard_map/all_to_all | solution.py:65
  47.9 2.4 %collective-permute-start.10 = (bf16[512,128]{0,1:T(8,128)(2,1)}, bf16[512,128]{0,1:T(8,128)(2,1)}, u32[]{:S(2)}, u32[]{:S(2)}) collective-permute-start(bf16[512,128]{0,1:T(8,128)(2,1)} %copy.131), channel_id=1, source_target_pairs={{1,0},{2,1},{3,2},{4,3},{5,4},{6,5},{7,6},{9,8},{10,9},{11,10},{12... | collective-permute-start | bytes 393224 | tf_op jit(solution)/shard_map/ppermute | solution.py:31
  50.3 4.3 %collective-permute-start.8 = (bf16[512,128]{0,1:T(8,128)(2,1)}, bf16[512,128]{0,1:T(8,128)(2,1)}, u32[]{:S(2)}, u32[]{:S(2)}) collective-permute-start(bf16[512,128]{0,1:T(8,128)(2,1)} %copy.131), channel_id=1, source_target_pairs={{0,1},{1,2},{2,3},{3,4},{4,5},{5,6},{6,7},{8,9},{9,10},{10,11},{11... | collective-permute-start | bytes 393224 | tf_op jit(solution)/shard_map/ppermute | solution.py:31
  56.1 1.9 collective-permute-start.6
  58.0 3.4 %all-to-all-start = ((bf16[4,2,16384]{2,1,0:T(2,128)(2,1)}), bf16[4,2,16384]{2,1,0:T(2,128)(2,1)S(1)}, u32[]{:S(2)}, u32[]{:S(2)}) async-start(bf16[4,2,16384]{2,1,0:T(2,128)(2,1)} %reshape.497), calls=%async_computation | async-start | bytes 524288 | tf_op jit(solution)/shard_map/all_to_all | solution.py:66
  62.0 4.8 %collective-permute-start.2 = (bf16[30,256]{1,0:T(8,128)(2,1)S(1)}, bf16[30,256]{1,0:T(8,128)(2,1)S(1)}, u32[]{:S(2)}, u32[]{:S(2)}) collective-permute-start(bf16[30,256]{1,0:T(8,128)(2,1)S(1)} %get-tuple-element.36), channel_id=1, source_target_pairs={{0,1},{1,2},{2,3},{3,4},{4,5},{5,6},{6,7},{8,9},{9,10},{10,11},{11... | collective-permute-start | bytes 46088 | tf_op jit(solution)/shard_map/ppermute | solution.py:19
  66.8 1.9 collective-permute-start.3
  69.3 4.8 %collective-permute-start = (bf16[30,256]{1,0:T(8,128)(2,1)S(1)}, bf16[30,256]{1,0:T(8,128)(2,1)S(1)}, u32[]{:S(2)}, u32[]{:S(2)}) collective-permute-start(bf16[30,256]{1,0:T(8,128)(2,1)S(1)} %get-tuple-element.38), channel_id=1, source_target_pairs={{0,1},{1,2},{2,3},{3,4},{4,5},{5,6},{6,7},{8,9},{9,10},{10,11},{11... | collective-permute-start | bytes 46088 | tf_op jit(solution)/shard_map/ppermute | solution.py:19
  74.1 1.9 collective-permute-start.1
  76.1 5.0 %collective-permute-start.4 = (bf16[512,128]{1,0:T(8,128)(2,1)}, bf16[512,128]{1,0:T(8,128)(2,1)}, u32[]{:S(2)}, u32[]{:S(2)}) collective-permute-start(bf16[512,128]{1,0:T(8,128)(2,1)} %bitcast.40), channel_id=1, source_target_pairs={{0,1},{1,2},{2,3},{3,4},{4,5},{5,6},{6,7},{8,9},{9,10},{10,11},{11... | collective-permute-start | bytes 393224 | tf_op jit(solution)/shard_map/ppermute | solution.py:31
  81.2 2.4 %slice_multiply_fusion.31 = f32[542,256]{1,0:T(8,128)S(1)} fusion(f32[572,256]{1,0:T(8,128)S(1)} %maximum_convert_fusion, f32[572,256]{1,0:T(8,128)S(1)} %maximum_convert_fusion.1, f32[256]{0:T(256)S(1)} %bitcast.217, f32[256]{0:T(256)S(1)} %bitcast.219, f32[256]{0:T(256)S(1)} %bitcast.221, f32[256]{0:T(256)S(1)} %bitcast.223, f32[256]{0:T(256)S(1)} %bitcast.225, ...), kind=kLoop, calls=%fused_computation.140 | loop fusion | flops 9573888 | bytes 18347008 | tf_op jit(solution)/shard_map/mul | solution.py:46
  83.6 2.8 %fusion.71 = bf16[512,256]{1,0:T(8,128)(2,1)} fusion(f32[542,256]{1,0:T(8,128)S(1)} %slice_multiply_fusion.31, f32[572,256]{1,0:T(8,128)S(1)} %maximum_convert_fusion, f32[256]{0:T(256)S(1)} %bitcast.218, f32[256]{0:T(256)S(1)} %bitcast.220, f32[256]{0:T(256)S(1)} %bitcast.222, f32[256]{0:T(256)S(1)} %bitcast.224, f32[256]{0:T(256)S(1)} %bitcast.226, ...), kind=kLoop, calls=%fused_computation.143 | loop fusion | flops 8257536 | bytes 17071104 | tf_op jit(solution)/shard_map/convert_element_type | solution.py:51
  86.5 1.6 fusion.115
  90.8 1.9 collective-permute-start.7
  92.8 1.7 copy.127
  94.5 4.9 %collective-permute-start.5 = (bf16[512,128]{1,0:T(8,128)(2,1)}, bf16[512,128]{1,0:T(8,128)(2,1)}, u32[]{:S(2)}, u32[]{:S(2)}) collective-permute-start(bf16[512,128]{1,0:T(8,128)(2,1)} %collective-permute-done.4), channel_id=1, source_target_pairs={{0,1},{1,2},{2,3},{3,4},{4,5},{5,6},{6,7},{8,9},{9,10},{10,11},{11... | collective-permute-start | bytes 393224 | tf_op jit(solution)/shard_map/ppermute | solution.py:31
  99.4 2.9 %fusion.113 = (f32[2,512]{1,0:T(2,128)S(1)}, f32[2,512,512]{1,2,0:T(8,128)}) fusion(bf16[512,2,64]{0,2,1:T(8,128)(2,1)S(1)} %reshape_squeeze.8, bf16[512,2,64]{0,2,1:T(8,128)(2,1)S(1)} %bitcast.209, pred[512,512]{0,1:T(8,128)(4,1)} %get-tuple-element.82), kind=kOutput, calls=%fused_computation.242 | convolution fusion | flops 68680704 | bytes 2625536 | tf_op jit(solution)/shard_map/qhd,khd->hqk/dot_general | solution.py:128
  102.3 1.9 fusion.114
  104.2 1.9 collective-permute-start.11
  106.2 4.8 %collective-permute-start.9 = (bf16[512,128]{0,1:T(8,128)(2,1)}, bf16[512,128]{0,1:T(8,128)(2,1)}, u32[]{:S(2)}, u32[]{:S(2)}) collective-permute-start(bf16[512,128]{0,1:T(8,128)(2,1)} %collective-permute-done.8), channel_id=1, source_target_pairs={{0,1},{1,2},{2,3},{3,4},{4,5},{5,6},{6,7},{8,9},{9,10},{10,11},{11... | collective-permute-start | bytes 393224 | tf_op jit(solution)/shard_map/ppermute | solution.py:31
  112.0 1.7 copy.126
  113.7 3.0 %fusion.116 = (f32[2,512]{1,0:T(2,128)S(1)}, f32[2,512,512]{1,2,0:T(8,128)}) fusion(bf16[512,2,64]{0,2,1:T(8,128)(2,1)S(1)} %reshape_squeeze.8, bf16[512,2,64]{0,2,1:T(8,128)(2,1)} %bitcast.211, pred[512,512]{0,1:T(8,128)(4,1)} %get-tuple-element.80), kind=kOutput, calls=%fused_computation.245 | convolution fusion | flops 68680704 | bytes 2625536 | tf_op jit(solution)/shard_map/qhd,khd->hqk/dot_general | solution.py:128
  116.8 2.0 %fusion.112 = (f32[2,512]{1,0:T(2,128)S(1)}, f32[2,512,512]{1,2,0:T(8,128)}) fusion(bf16[512,2,64]{0,2,1:T(8,128)(2,1)S(1)} %reshape_squeeze.8, bf16[512,2,64]{0,2,1:T(8,128)(2,1)S(1)} %bitcast.197, pred[512,512]{0,1:T(8,128)(4,1)S(1)} %copy-done.23), kind=kOutput, calls=%fused_computation.241 | convolution fusion | flops 68680704 | bytes 2625536 | tf_op jit(solution)/shard_map/qhd,khd->hqk/dot_general | solution.py:128
  118.8 1.7 convolution_convert_fusion.5
  122.2 1.7 multiply_reduce_fusion
  123.8 1.7 multiply_reduce_fusion.1
  125.5 1.7 multiply_reduce_fusion.2
  127.2 1.5 multiply_reduce_fusion.3
  129.9 1.1 convolution_convert_fusion.2
  131.0 1.1 convolution_convert_fusion.1
  132.1 1.1 convolution_convert_fusion
  133.2 1.2 fusion.12
  134.4 4.2 %multiply_convert_fusion = (bf16[2,512,512]{1,2,0:T(8,128)(2,1)}, bf16[2,512,512]{1,2,0:T(8,128)(2,1)}, bf16[2,512,512]{1,2,0:T(8,128)(2,1)}, bf16[2,512,512]{1,2,0:T(8,128)(2,1)S(1)}, bf16[2,512,512]{1,2,0:T(8,128)(2,1)}) fusion(f32[2,512,512]{1,2,0:T(8,128)S(1)} %get-tuple-element.100, f32[2,512,512]{1,2,0:T(8,128)S(1)} %copy-done.4, ...), kind=kLoop, calls=%fused_computation | loop fusion | flops 10485760 | bytes 26222592 | tf_op jit(solution)/shard_map/convert_element_type | solution.py:162
  143.9 1.1 fusion.18
  145.0 1.7 copy.147
  146.8 2.3 %fusion.15 = bf16[2,512,64]{1,2,0:T(8,128)(2,1)} fusion(bf16[2,512,512]{1,2,0:T(8,128)(2,1)} %get-tuple-element.76, bf16[512,2,64]{0,2,1:T(8,128)(2,1)S(1)} %reshape_squeeze.8), kind=kOutput, calls=%fused_computation.54 | convolution fusion | flops 67239936 | bytes 1310720 | tf_op jit(solution)/shard_map/hqk,qhd->khd/dot_general | solution.py:171
  149.1 1.7 copy.140
  150.8 2.3 %fusion.16 = bf16[2,512,64]{1,2,0:T(8,128)(2,1)} fusion(bf16[2,512,512]{1,2,0:T(8,128)(2,1)} %get-tuple-element.77, bf16[512,2,64]{0,2,1:T(8,128)(2,1)S(1)} %reshape_squeeze.8), kind=kOutput, calls=%fused_computation.55 | convolution fusion | flops 67239936 | bytes 1310720 | tf_op jit(solution)/shard_map/hqk,qhd->khd/dot_general | solution.py:171
  153.1 1.7 copy.143
  154.7 1.7 copy.145
  156.4 1.3 fusion.117
  157.7 1.6 convolution_add_fusion.2
  160.7 1.7 copy.158
  162.3 2.0 %collective-permute-start.14 = (bf16[512,128]{1,0:T(8,128)(2,1)}, bf16[512,128]{1,0:T(8,128)(2,1)S(1)}, u32[]{:S(2)}, u32[]{:S(2)}) collective-permute-start(bf16[512,128]{1,0:T(8,128)(2,1)} %copy.145), channel_id=1, source_target_pairs={{0,1},{1,2},{2,3},{3,4},{4,5},{5,6},{6,7},{8,9},{9,10},{10,11},{11... | collective-permute-start | bytes 393224 | tf_op jit(solution)/shard_map/ppermute | solution.py:31
  164.4 3.8 %collective-permute-start.13 = (bf16[512,128]{1,0:T(8,128)(2,1)}, bf16[512,128]{1,0:T(8,128)(2,1)S(1)}, u32[]{:S(2)}, u32[]{:S(2)}) collective-permute-start(bf16[512,128]{1,0:T(8,128)(2,1)} %copy.143), channel_id=1, source_target_pairs={{1,0},{2,1},{3,2},{4,3},{5,4},{6,5},{7,6},{9,8},{10,9},{11,10},{12... | collective-permute-start | bytes 393224 | tf_op jit(solution)/shard_map/ppermute | solution.py:31
  168.2 2.4 %collective-permute-start.12 = (bf16[512,128]{1,0:T(8,128)(2,1)}, bf16[512,128]{1,0:T(8,128)(2,1)S(1)}, u32[]{:S(2)}, u32[]{:S(2)}) collective-permute-start(bf16[512,128]{1,0:T(8,128)(2,1)} %copy.140), channel_id=1, source_target_pairs={{2,0},{3,1},{4,2},{5,3},{6,4},{7,5},{10,8},{11,9},{12,10},{13,11},... | collective-permute-start | bytes 393224 | tf_op jit(solution)/shard_map/ppermute | solution.py:31
  170.6 3.5 %collective-permute-start.15 = (bf16[512,128]{1,0:T(8,128)(2,1)}, bf16[512,128]{1,0:T(8,128)(2,1)S(1)}, u32[]{:S(2)}, u32[]{:S(2)}) collective-permute-start(bf16[512,128]{1,0:T(8,128)(2,1)} %copy.147), channel_id=1, source_target_pairs={{0,2},{1,3},{2,4},{3,5},{4,6},{5,7},{8,10},{9,11},{10,12},{11,13},... | collective-permute-start | bytes 393224 | tf_op jit(solution)/shard_map/ppermute | solution.py:31
  174.6 2.4 %collective-permute-start.16 = (bf16[512,128]{1,0:T(8,128)(2,1)}, bf16[512,128]{1,0:T(8,128)(2,1)S(1)}, u32[]{:S(2)}, u32[]{:S(2)}) collective-permute-start(bf16[512,128]{1,0:T(8,128)(2,1)} %copy.150), channel_id=1, source_target_pairs={{2,0},{3,1},{4,2},{5,3},{6,4},{7,5},{10,8},{11,9},{12,10},{13,11},... | collective-permute-start | bytes 393224 | tf_op jit(solution)/shard_map/ppermute | solution.py:31
  177.0 1.9 collective-permute-start.17
  178.9 4.8 %collective-permute-start.18 = (bf16[512,128]{1,0:T(8,128)(2,1)}, bf16[512,128]{1,0:T(8,128)(2,1)S(1)}, u32[]{:S(2)}, u32[]{:S(2)}) collective-permute-start(bf16[512,128]{1,0:T(8,128)(2,1)} %copy.155), channel_id=1, source_target_pairs={{0,1},{1,2},{2,3},{3,4},{4,5},{5,6},{6,7},{8,9},{9,10},{10,11},{11... | collective-permute-start | bytes 393224 | tf_op jit(solution)/shard_map/ppermute | solution.py:31
  183.8 3.5 %collective-permute-start.19 = (bf16[512,128]{1,0:T(8,128)(2,1)}, bf16[512,128]{1,0:T(8,128)(2,1)S(1)}, u32[]{:S(2)}, u32[]{:S(2)}) collective-permute-start(bf16[512,128]{1,0:T(8,128)(2,1)} %copy.157), channel_id=1, source_target_pairs={{0,2},{1,3},{2,4},{3,5},{4,6},{5,7},{8,10},{9,11},{10,12},{11,13},... | collective-permute-start | bytes 393224 | tf_op jit(solution)/shard_map/ppermute | solution.py:31
  188.0 2.8 %collective-permute-done.19 = bf16[512,128]{1,0:T(8,128)(2,1)S(1)} collective-permute-done((bf16[512,128]{1,0:T(8,128)(2,1)}, bf16[512,128]{1,0:T(8,128)(2,1)S(1)}, u32[]{:S(2)}, u32[]{:S(2)}) %collective-permute-start.19) | collective-permute-done | bytes 131104 | tf_op jit(solution)/shard_map/ppermute | solution.py:31
  (140 shorter events, 26.0 us)
Async XLA Ops:
  7.2 111.7 %copy-start = (bf16[512,1024]{1,0:T(8,128)(2,1)S(1)}, bf16[512,1024]{1,0:T(8,128)(2,1)}, u32[]{:S(2)}) copy-start(bf16[512,1024]{1,0:T(8,128)(2,1)} %param.13) | copy-start | bytes 3145732
  7.2 13.3 %copy-start.25 = (bf16[1,128,512]{2,1,0:T(8,128)(2,1)S(1)}, bf16[1,128,512]{2,1,0:T(8,128)(2,1)}, u32[]{:S(2)}) copy-start(bf16[1,128,512]{2,1,0:T(8,128)(2,1)} %param.8) | copy-start | bytes 393220
  7.2 16.1 %copy-start.26 = (bf16[1,128,512]{2,1,0:T(8,128)(2,1)S(1)}, bf16[1,128,512]{2,1,0:T(8,128)(2,1)}, u32[]{:S(2)}) copy-start(bf16[1,128,512]{2,1,0:T(8,128)(2,1)} %param.9) | copy-start | bytes 393220
  8.8 16.8 %all-to-all-start.4 = ((bf16[4,1,128,128]{3,2,1,0:T(8,128)(2,1)}), bf16[4,1,128,128]{3,2,1,0:T(8,128)(2,1)S(1)}, u32[]{:S(2)}, u32[]{:S(2)}) async-start(bf16[4,1,128,128]{3,2,1,0:T(8,128)(2,1)} %pad_maximum_fusion), calls=%async_computation.4 | async-start | bytes 262144 | tf_op jit(solution)/shard_map/all_to_all | solution.py:62
  12.6 24.3 %copy-start.21 = (bf16[1,128,1024]{2,1,0:T(8,128)(2,1)S(1)}, bf16[1,128,1024]{2,1,0:T(8,128)(2,1)}, u32[]{:S(2)}) copy-start(bf16[1,128,1024]{2,1,0:T(8,128)(2,1)} %param.11) | copy-start | bytes 786436
  22.6 17.7 %copy-start.22 = (bf16[1,128,1024]{2,1,0:T(8,128)(2,1)S(1)}, bf16[1,128,1024]{2,1,0:T(8,128)(2,1)}, u32[]{:S(2)}) copy-start(bf16[1,128,1024]{2,1,0:T(8,128)(2,1)} %param.12) | copy-start | bytes 786436
  25.6 6.4 %all-to-all-start.2 = ((bf16[4,2,8192]{2,1,0:T(2,128)(2,1)}), bf16[4,2,8192]{2,1,0:T(2,128)(2,1)S(1)}, u32[]{:S(2)}, u32[]{:S(2)}) async-start(bf16[4,2,8192]{2,1,0:T(2,128)(2,1)} %reshape.503), calls=%async_computation.2 | async-start | bytes 262144 | tf_op jit(solution)/shard_map/all_to_all | solution.py:59
  31.9 11.8 %all-to-all-start.3 = ((bf16[4,2,8192]{2,1,0:T(2,128)(2,1)}), bf16[4,2,8192]{2,1,0:T(2,128)(2,1)S(1)}, u32[]{:S(2)}, u32[]{:S(2)}) async-start(bf16[4,2,8192]{2,1,0:T(2,128)(2,1)} %reshape.501), calls=%async_computation.3 | async-start | bytes 262144 | tf_op jit(solution)/shard_map/all_to_all | solution.py:60
  43.7 14.3 %all-to-all-start.1 = ((bf16[4,2,16384]{2,1,0:T(2,128)(2,1)}), bf16[4,2,16384]{2,1,0:T(2,128)(2,1)S(1)}, u32[]{:S(2)}, u32[]{:S(2)}) async-start(bf16[4,2,16384]{2,1,0:T(2,128)(2,1)} %reshape.499), calls=%async_computation.1 | async-start | bytes 524288 | tf_op jit(solution)/shard_map/all_to_all | solution.py:65
  47.9 56.3 %collective-permute-start.10 = (bf16[512,128]{0,1:T(8,128)(2,1)}, bf16[512,128]{0,1:T(8,128)(2,1)}, u32[]{:S(2)}, u32[]{:S(2)}) collective-permute-start(bf16[512,128]{0,1:T(8,128)(2,1)} %copy.131), channel_id=1, source_target_pairs={{1,0},{2,1},{3,2},{4,3},{5,4},{6,5},{7,6},{9,8},{10,9},{11,10},{12... | collective-permute-start | bytes 393224 | tf_op jit(solution)/shard_map/ppermute | solution.py:31
  50.3 55.8 %collective-permute-start.8 = (bf16[512,128]{0,1:T(8,128)(2,1)}, bf16[512,128]{0,1:T(8,128)(2,1)}, u32[]{:S(2)}, u32[]{:S(2)}) collective-permute-start(bf16[512,128]{0,1:T(8,128)(2,1)} %copy.131), channel_id=1, source_target_pairs={{0,1},{1,2},{2,3},{3,4},{4,5},{5,6},{6,7},{8,9},{9,10},{10,11},{11... | collective-permute-start | bytes 393224 | tf_op jit(solution)/shard_map/ppermute | solution.py:31
  56.1 30.4 %copy-start.16 = (bf16[512,2,64]{0,2,1:T(8,128)(2,1)}, bf16[512,2,64]{0,2,1:T(8,128)(2,1)S(1)}, u32[]{:S(2)}) copy-start(bf16[512,2,64]{0,2,1:T(8,128)(2,1)S(1)} %reshape_squeeze.9) | copy-start | bytes 393220
  56.1 33.7 %collective-permute-start.6 = (bf16[512,128]{1,0:T(8,128)(2,1)}, bf16[512,128]{1,0:T(8,128)(2,1)}, u32[]{:S(2)}, u32[]{:S(2)}) collective-permute-start(bf16[512,128]{1,0:T(8,128)(2,1)} %bitcast.40), channel_id=1, source_target_pairs={{1,0},{2,1},{3,2},{4,3},{5,4},{6,5},{7,6},{9,8},{10,9},{11,10},{12... | collective-permute-start | bytes 393224 | tf_op jit(solution)/shard_map/ppermute | solution.py:31
  58.0 10.7 %all-to-all-start = ((bf16[4,2,16384]{2,1,0:T(2,128)(2,1)}), bf16[4,2,16384]{2,1,0:T(2,128)(2,1)S(1)}, u32[]{:S(2)}, u32[]{:S(2)}) async-start(bf16[4,2,16384]{2,1,0:T(2,128)(2,1)} %reshape.497), calls=%async_computation | async-start | bytes 524288 | tf_op jit(solution)/shard_map/all_to_all | solution.py:66
  61.4 57.4 %all-gather.2.cloned.1.call-start = ((), (), s32[]{:S(2)}) async-start(), calls=%async_computation.5 | async-start | bytes 1310720 | tf_op jit(solution)/shard_map/all_gather | solution.py:88
  62.0 7.3 %collective-permute-start.2 = (bf16[30,256]{1,0:T(8,128)(2,1)S(1)}, bf16[30,256]{1,0:T(8,128)(2,1)S(1)}, u32[]{:S(2)}, u32[]{:S(2)}) collective-permute-start(bf16[30,256]{1,0:T(8,128)(2,1)S(1)} %get-tuple-element.36), channel_id=1, source_target_pairs={{0,1},{1,2},{2,3},{3,4},{4,5},{5,6},{6,7},{8,9},{9,10},{10,11},{11... | collective-permute-start | bytes 46088 | tf_op jit(solution)/shard_map/ppermute | solution.py:19
  66.8 7.3 %collective-permute-start.3 = (bf16[30,256]{1,0:T(8,128)(2,1)S(1)}, bf16[30,256]{1,0:T(8,128)(2,1)S(1)}, u32[]{:S(2)}, u32[]{:S(2)}) collective-permute-start(bf16[30,256]{1,0:T(8,128)(2,1)S(1)} %get-tuple-element.37), channel_id=1, source_target_pairs={{1,0},{2,1},{3,2},{4,3},{5,4},{6,5},{7,6},{9,8},{10,9},{11,10},{12... | collective-permute-start | bytes 46088 | tf_op jit(solution)/shard_map/ppermute | solution.py:21
  69.3 6.8 %collective-permute-start = (bf16[30,256]{1,0:T(8,128)(2,1)S(1)}, bf16[30,256]{1,0:T(8,128)(2,1)S(1)}, u32[]{:S(2)}, u32[]{:S(2)}) collective-permute-start(bf16[30,256]{1,0:T(8,128)(2,1)S(1)} %get-tuple-element.38), channel_id=1, source_target_pairs={{0,1},{1,2},{2,3},{3,4},{4,5},{5,6},{6,7},{8,9},{9,10},{10,11},{11... | collective-permute-start | bytes 46088 | tf_op jit(solution)/shard_map/ppermute | solution.py:19
  74.1 7.0 %collective-permute-start.1 = (bf16[30,256]{1,0:T(8,128)(2,1)S(1)}, bf16[30,256]{1,0:T(8,128)(2,1)S(1)}, u32[]{:S(2)}, u32[]{:S(2)}) collective-permute-start(bf16[30,256]{1,0:T(8,128)(2,1)S(1)} %get-tuple-element.39), channel_id=1, source_target_pairs={{1,0},{2,1},{3,2},{4,3},{5,4},{6,5},{7,6},{9,8},{10,9},{11,10},{12... | collective-permute-start | bytes 46088 | tf_op jit(solution)/shard_map/ppermute | solution.py:21
  76.1 16.7 %collective-permute-start.4 = (bf16[512,128]{1,0:T(8,128)(2,1)}, bf16[512,128]{1,0:T(8,128)(2,1)}, u32[]{:S(2)}, u32[]{:S(2)}) collective-permute-start(bf16[512,128]{1,0:T(8,128)(2,1)} %bitcast.40), channel_id=1, source_target_pairs={{0,1},{1,2},{2,3},{3,4},{4,5},{5,6},{6,7},{8,9},{9,10},{10,11},{11... | collective-permute-start | bytes 393224 | tf_op jit(solution)/shard_map/ppermute | solution.py:31
  90.8 13.4 %copy-start.17 = (bf16[512,128]{0,1:T(8,128)(2,1)}, bf16[512,128]{0,1:T(8,128)(2,1)S(1)}, u32[]{:S(2)}) copy-start(bf16[512,128]{0,1:T(8,128)(2,1)S(1)} %copy.128) | copy-start | bytes 393220
  90.8 20.1 %collective-permute-start.7 = (bf16[512,128]{1,0:T(8,128)(2,1)}, bf16[512,128]{1,0:T(8,128)(2,1)}, u32[]{:S(2)}, u32[]{:S(2)}) collective-permute-start(bf16[512,128]{1,0:T(8,128)(2,1)} %collective-permute-done.6), channel_id=1, source_target_pairs={{1,0},{2,1},{3,2},{4,3},{5,4},{6,5},{7,6},{9,8},{10,9},{11,10},{12... | collective-permute-start | bytes 393224 | tf_op jit(solution)/shard_map/ppermute | solution.py:31
  94.5 7.8 %copy-start.19 = (bf16[512,128]{0,1:T(8,128)(2,1)S(1)}, bf16[512,128]{0,1:T(8,128)(2,1)}, u32[]{:S(2)}) copy-start(bf16[512,128]{0,1:T(8,128)(2,1)} %copy.127) | copy-start | bytes 393220
  94.5 7.9 %copy-start.24 = (pred[512,512]{0,1:T(8,128)(4,1)S(1)}, pred[512,512]{0,1:T(8,128)(4,1)}, u32[]{:S(2)}) copy-start(pred[512,512]{0,1:T(8,128)(4,1)} %get-tuple-element.81) | copy-start | bytes 786436
  94.5 17.6 %collective-permute-start.5 = (bf16[512,128]{1,0:T(8,128)(2,1)}, bf16[512,128]{1,0:T(8,128)(2,1)}, u32[]{:S(2)}, u32[]{:S(2)}) collective-permute-start(bf16[512,128]{1,0:T(8,128)(2,1)} %collective-permute-done.4), channel_id=1, source_target_pairs={{0,1},{1,2},{2,3},{3,4},{4,5},{5,6},{6,7},{8,9},{9,10},{10,11},{11... | collective-permute-start | bytes 393224 | tf_op jit(solution)/shard_map/ppermute | solution.py:31
  104.2 17.0 %collective-permute-start.11 = (bf16[512,128]{0,1:T(8,128)(2,1)}, bf16[512,128]{0,1:T(8,128)(2,1)}, u32[]{:S(2)}, u32[]{:S(2)}) collective-permute-start(bf16[512,128]{0,1:T(8,128)(2,1)} %collective-permute-done.10), channel_id=1, source_target_pairs={{1,0},{2,1},{3,2},{4,3},{5,4},{6,5},{7,6},{9,8},{10,9},{11,10},{12... | collective-permute-start | bytes 393224 | tf_op jit(solution)/shard_map/ppermute | solution.py:31
  106.2 21.0 %collective-permute-start.9 = (bf16[512,128]{0,1:T(8,128)(2,1)}, bf16[512,128]{0,1:T(8,128)(2,1)}, u32[]{:S(2)}, u32[]{:S(2)}) collective-permute-start(bf16[512,128]{0,1:T(8,128)(2,1)} %collective-permute-done.8), channel_id=1, source_target_pairs={{0,1},{1,2},{2,3},{3,4},{4,5},{5,6},{6,7},{8,9},{9,10},{10,11},{11... | collective-permute-start | bytes 393224 | tf_op jit(solution)/shard_map/ppermute | solution.py:31
  112.0 6.8 %copy-start.10 = (bf16[512,128]{0,1:T(8,128)(2,1)}, bf16[512,128]{0,1:T(8,128)(2,1)S(1)}, u32[]{:S(2)}) copy-start(bf16[512,128]{0,1:T(8,128)(2,1)S(1)} %copy.129) | copy-start | bytes 393220
  113.7 3.0 %copy-start.23 = (pred[512,512]{0,1:T(8,128)(4,1)S(1)}, pred[512,512]{0,1:T(8,128)(4,1)}, u32[]{:S(2)}) copy-start(pred[512,512]{0,1:T(8,128)(4,1)} %get-tuple-element.83) | copy-start | bytes 786436
  120.6 1.6 copy-start.4
  122.1 1.7 copy-start.1
  123.8 1.7 copy-start.2
  125.5 1.7 copy-start.3
  134.4 5.4 %copy-start.18 = (bf16[512,128]{0,1:T(8,128)(2,1)S(1)}, bf16[512,128]{0,1:T(8,128)(2,1)}, u32[]{:S(2)}) copy-start(bf16[512,128]{0,1:T(8,128)(2,1)} %copy-done.17) | copy-start | bytes 393220
  138.6 2.1 %copy-start.8 = (f32[2,64,512]{2,1,0:T(8,128)S(1)}, f32[2,64,512]{2,1,0:T(8,128)}, u32[]{:S(2)}) copy-start(f32[2,64,512]{2,1,0:T(8,128)} %fusion.12) | copy-start | bytes 786436
  138.6 2.3 %copy-start.15 = (bf16[2,64,512]{2,1,0:T(8,128)(2,1)S(1)}, bf16[2,64,512]{2,1,0:T(8,128)(2,1)}, u32[]{:S(2)}) copy-start(bf16[2,64,512]{2,1,0:T(8,128)(2,1)} %convolution_convert_fusion) | copy-start | bytes 393220
  138.6 3.0 %copy-start.14 = (bf16[2,64,512]{2,1,0:T(8,128)(2,1)S(1)}, bf16[2,64,512]{2,1,0:T(8,128)(2,1)}, u32[]{:S(2)}) copy-start(bf16[2,64,512]{2,1,0:T(8,128)(2,1)} %convolution_convert_fusion.1) | copy-start | bytes 393220
  138.6 3.8 %copy-start.13 = (bf16[2,64,512]{2,1,0:T(8,128)(2,1)S(1)}, bf16[2,64,512]{2,1,0:T(8,128)(2,1)}, u32[]{:S(2)}) copy-start(bf16[2,64,512]{2,1,0:T(8,128)(2,1)} %convolution_convert_fusion.2) | copy-start | bytes 393220
  138.6 4.6 %copy-start.12 = (bf16[2,64,512]{2,1,0:T(8,128)(2,1)S(1)}, bf16[2,64,512]{2,1,0:T(8,128)(2,1)}, u32[]{:S(2)}) copy-start(bf16[2,64,512]{2,1,0:T(8,128)(2,1)} %convolution_convert_fusion.3) | copy-start | bytes 393220
  138.6 5.3 %copy-start.6 = (bf16[2,512,512]{1,2,0:T(8,128)(2,1)S(1)}, bf16[2,512,512]{1,2,0:T(8,128)(2,1)}, u32[]{:S(2)}) copy-start(bf16[2,512,512]{1,2,0:T(8,128)(2,1)} %get-tuple-element.75) | copy-start | bytes 3145732
  145.0 11.4 %copy-start.5 = (bf16[2,512,512]{1,2,0:T(8,128)(2,1)S(1)}, bf16[2,512,512]{1,2,0:T(8,128)(2,1)}, u32[]{:S(2)}) copy-start(bf16[2,512,512]{1,2,0:T(8,128)(2,1)} %get-tuple-element.79) | copy-start | bytes 3145732
  156.4 3.0 %copy-start.7 = (bf16[2,512,512]{1,2,0:T(8,128)(2,1)S(1)}, bf16[2,512,512]{1,2,0:T(8,128)(2,1)}, u32[]{:S(2)}) copy-start(bf16[2,512,512]{1,2,0:T(8,128)(2,1)} %get-tuple-element.77) | copy-start | bytes 3145732
  156.4 3.0 %copy-start.9 = (f32[2,512,64]{1,2,0:T(8,128)S(1)}, f32[2,512,64]{1,2,0:T(8,128)}, u32[]{:S(2)}) copy-start(f32[2,512,64]{1,2,0:T(8,128)} %fusion.118) | copy-start | bytes 786436
  156.4 3.0 %copy-start.20 = (bf16[512,128]{0,1:T(8,128)(2,1)S(1)}, bf16[512,128]{0,1:T(8,128)(2,1)}, u32[]{:S(2)}) copy-start(bf16[512,128]{0,1:T(8,128)(2,1)} %copy.127) | copy-start | bytes 393220
  157.7 2.0 copy-start.11
  162.3 14.7 %collective-permute-start.14 = (bf16[512,128]{1,0:T(8,128)(2,1)}, bf16[512,128]{1,0:T(8,128)(2,1)S(1)}, u32[]{:S(2)}, u32[]{:S(2)}) collective-permute-start(bf16[512,128]{1,0:T(8,128)(2,1)} %copy.145), channel_id=1, source_target_pairs={{0,1},{1,2},{2,3},{3,4},{4,5},{5,6},{6,7},{8,9},{9,10},{10,11},{11... | collective-permute-start | bytes 393224 | tf_op jit(solution)/shard_map/ppermute | solution.py:31
  164.4 14.6 %collective-permute-start.13 = (bf16[512,128]{1,0:T(8,128)(2,1)}, bf16[512,128]{1,0:T(8,128)(2,1)S(1)}, u32[]{:S(2)}, u32[]{:S(2)}) collective-permute-start(bf16[512,128]{1,0:T(8,128)(2,1)} %copy.143), channel_id=1, source_target_pairs={{1,0},{2,1},{3,2},{4,3},{5,4},{6,5},{7,6},{9,8},{10,9},{11,10},{12... | collective-permute-start | bytes 393224 | tf_op jit(solution)/shard_map/ppermute | solution.py:31
  168.2 15.6 %collective-permute-start.12 = (bf16[512,128]{1,0:T(8,128)(2,1)}, bf16[512,128]{1,0:T(8,128)(2,1)S(1)}, u32[]{:S(2)}, u32[]{:S(2)}) collective-permute-start(bf16[512,128]{1,0:T(8,128)(2,1)} %copy.140), channel_id=1, source_target_pairs={{2,0},{3,1},{4,2},{5,3},{6,4},{7,5},{10,8},{11,9},{12,10},{13,11},... | collective-permute-start | bytes 393224 | tf_op jit(solution)/shard_map/ppermute | solution.py:31
  170.6 16.7 %collective-permute-start.15 = (bf16[512,128]{1,0:T(8,128)(2,1)}, bf16[512,128]{1,0:T(8,128)(2,1)S(1)}, u32[]{:S(2)}, u32[]{:S(2)}) collective-permute-start(bf16[512,128]{1,0:T(8,128)(2,1)} %copy.147), channel_id=1, source_target_pairs={{0,2},{1,3},{2,4},{3,5},{4,6},{5,7},{8,10},{9,11},{10,12},{11,13},... | collective-permute-start | bytes 393224 | tf_op jit(solution)/shard_map/ppermute | solution.py:31
  174.6 13.4 %collective-permute-start.16 = (bf16[512,128]{1,0:T(8,128)(2,1)}, bf16[512,128]{1,0:T(8,128)(2,1)S(1)}, u32[]{:S(2)}, u32[]{:S(2)}) collective-permute-start(bf16[512,128]{1,0:T(8,128)(2,1)} %copy.150), channel_id=1, source_target_pairs={{2,0},{3,1},{4,2},{5,3},{6,4},{7,5},{10,8},{11,9},{12,10},{13,11},... | collective-permute-start | bytes 393224 | tf_op jit(solution)/shard_map/ppermute | solution.py:31
  177.0 11.0 %collective-permute-start.17 = (bf16[512,128]{1,0:T(8,128)(2,1)}, bf16[512,128]{1,0:T(8,128)(2,1)S(1)}, u32[]{:S(2)}, u32[]{:S(2)}) collective-permute-start(bf16[512,128]{1,0:T(8,128)(2,1)} %copy.153), channel_id=1, source_target_pairs={{1,0},{2,1},{3,2},{4,3},{5,4},{6,5},{7,6},{9,8},{10,9},{11,10},{12... | collective-permute-start | bytes 393224 | tf_op jit(solution)/shard_map/ppermute | solution.py:31
  178.9 9.1 %collective-permute-start.18 = (bf16[512,128]{1,0:T(8,128)(2,1)}, bf16[512,128]{1,0:T(8,128)(2,1)S(1)}, u32[]{:S(2)}, u32[]{:S(2)}) collective-permute-start(bf16[512,128]{1,0:T(8,128)(2,1)} %copy.155), channel_id=1, source_target_pairs={{0,1},{1,2},{2,3},{3,4},{4,5},{5,6},{6,7},{8,9},{9,10},{10,11},{11... | collective-permute-start | bytes 393224 | tf_op jit(solution)/shard_map/ppermute | solution.py:31
  183.8 7.1 %collective-permute-start.19 = (bf16[512,128]{1,0:T(8,128)(2,1)}, bf16[512,128]{1,0:T(8,128)(2,1)S(1)}, u32[]{:S(2)}, u32[]{:S(2)}) collective-permute-start(bf16[512,128]{1,0:T(8,128)(2,1)} %copy.157), channel_id=1, source_target_pairs={{0,2},{1,3},{2,4},{3,5},{4,6},{5,7},{8,10},{9,11},{10,12},{11,13},... | collective-permute-start | bytes 393224 | tf_op jit(solution)/shard_map/ppermute | solution.py:31
Sparse Core Ops, SparseCore 0:
  86.6 16.0 all-gather.1
